TPU v7x, 128 devices: a whole 4x4x4 slice. The times are simulated.
128 devices in a mesh: gx: 8 (over y, core), gy: 16 (over z, x).
Axes of the slice: x: 4, y: 4, z: 4, core: 2. Of those that a mesh axis runs over, the one named last changes fastest.
Arguments:
- velocity: float32 [3, 768, 512, 256], P(None, 'gx', 'gy'), may hold values from -6 to 6
- inflow: float32 [3, 512, 256], P(None, 'gy'), may hold values from -5 to 5
- positions: int32 [8, 64, 3, 256], P('gx'), may hold values from 0 to 765, as said below
- tiles: int32 [8, 64, 2], P('gx'), may hold values from 0 to 15, as said below
- coefs: float32 [8, 64, 256], P('gx'), may hold values from 2 to 20
- counts: int32 [8], P('gx'), may hold values from 1 to 64, as said below
Outputs:
- velocity_next: float32 [3, 768, 512, 256], P(None, 'gx', 'gy')
- blade_force: float32 [8, 64, 3, 256], P('gx')
Inputs may be any that keep to these rules, and one draw needn't show every extreme that they name: `positions`: for a record of tile row r, coordinate 0 is one value for all its points, from r * 96 + 2 to r * 96 + 93; coordinate 2 lies from 2 to 253; the points of a record lie on a straight segment in y and z. tiles[r, s, 1] is 2 or 3; the first listed y tile is the lowest y tile that holds a cell within 2 in y of some point of the record, or the tile after it. Records of row r with index below counts[r] are live; some row is full and some row has one live record.
All inputs are finite; a program needn't handle non-finite values.
Results may differ from a plain program's by a relative error of at most 0.00008.
Values sent between devices are 32-bit elements; how exact they have to be, the bound alone decides.
A program may use at most 128 MiB of HBM per device.

v0:
```python
import jax
import jax.numpy as jnp
from jax import lax
from jax.sharding import PartitionSpec as P

REC_ROW = 64
RAD = 2


VISCOSITY = 0.05
TIME_STEP = 0.1
WIDTH_EPS = 1.5
ROOT_PI = 1.7724538509055159


def padded(block, sides, width, periodic):
    for axis, dim in sides:
        count = lax.axis_size(axis)
        forward = [(i, i + 1) for i in range(count - 1)]
        if periodic:
            forward.append((count - 1, 0))
        backward = [(target, source) for source, target in forward]
        low = lax.ppermute(
            lax.slice_in_dim(block, block.shape[dim] - width, None, axis=dim), axis, forward
        )
        high = lax.ppermute(lax.slice_in_dim(block, 0, width, axis=dim), axis, backward)
        block = jnp.concatenate([low, block, high], axis=dim)
    return block


def kernel_weight(offset):
    inside = jnp.abs(offset) <= RAD
    dist = offset.astype(jnp.float32)
    value = jnp.exp(-((dist / WIDTH_EPS) ** 2)) / (WIDTH_EPS * ROOT_PI)
    return jnp.where(inside, value, jnp.zeros_like(value))


def tendency(field, inflow, force):
    tile_x = lax.axis_index("gx")
    last_x = lax.axis_size("gx") - 1
    xhalo = padded(field, (("gx", 1),), 1, False)
    west_ghost = jnp.where(tile_x == 0, inflow[:, None], xhalo[:, :1])
    east_ghost = jnp.where(tile_x == last_x, field[:, -1:], xhalo[:, -1:])
    xpad = jnp.concatenate([west_ghost, field, east_ghost], axis=1)
    ypad = padded(field, (("gy", 2),), 1, True)
    zpad = jnp.pad(field, ((0, 0), (0, 0), (0, 0), (1, 1)))
    east, west = (xpad[:, 2:], xpad[:, :-2])
    north, south = (ypad[:, :, 2:], ypad[:, :, :-2])
    upper, lower = (zpad[:, :, :, 2:], zpad[:, :, :, :-2])
    advect = (
        field[0:1] * (east - west) * 0.5
        + field[1:2] * (north - south) * 0.5
        + field[2:3] * (upper - lower) * 0.5
    )
    diffuse = east + west + north + south + upper + lower - 6.0 * field
    return -advect + VISCOSITY * diffuse + force


def force_law(sampled, strength):
    speed_norm = jnp.sqrt(jnp.sum(sampled * sampled, axis=0))
    return -strength * speed_norm * sampled


def forcing(field, positions, tiles, coefs, counts):
    highest = lax.Precision.HIGHEST
    tile_x = lax.axis_index("gx")
    tile_y = lax.axis_index("gy")
    groups_y = lax.axis_size("gy")
    cells_x = field.shape[1]
    cells_y = field.shape[2]
    depth = field.shape[3]
    total_y = cells_y * groups_y
    record = positions[0]
    hub_x = record[:, 0, 0] - tile_x * cells_x
    point_y = record[:, 1, :]
    point_z = record[:, 2, :]
    first_tile = tiles[0, :, 0]
    tile_count = tiles[0, :, 1]
    listed = ((tile_y - first_tile) % groups_y < tile_count).astype(jnp.float32)
    along_x = kernel_weight(jnp.arange(cells_x, dtype=jnp.int32)[None, :] - hub_x[:, None])
    cell_y = tile_y * cells_y + jnp.arange(cells_y, dtype=jnp.int32)
    dist_y = (cell_y[None, :, None] - point_y[:, None, :] + total_y // 2) % total_y - total_y // 2
    along_y = kernel_weight(dist_y) * listed[:, None, None]
    along_z = kernel_weight(jnp.arange(depth, dtype=jnp.int32)[None, None, :] - point_z[:, :, None])
    planes = jnp.einsum("ri,cijk->rcjk", along_x, field, precision=highest)
    inner_sums = jnp.einsum("rcjk,rpk->rcjp", planes, along_z, precision=highest)
    partial_value = jnp.einsum("rcjp,rjp->crp", inner_sums, along_y, precision=highest)
    live_mask = (jnp.arange(REC_ROW, dtype=jnp.int32) < counts[0]).astype(jnp.float32)
    strength = coefs[0] * live_mask[:, None]
    sampled = lax.psum(partial_value, "gy")
    point_force = force_law(sampled, strength)
    weighted = along_y[None] * point_force[:, :, None, :]
    force_slab = jnp.einsum("crjp,rpk->rcjk", weighted, along_z, precision=highest)
    grid_force = jnp.einsum("ri,rcjk->cijk", along_x, force_slab, precision=highest)
    return (grid_force, point_force)


def local(velocity, inflow, positions, tiles, coefs, counts):
    force_a, points_a = forcing(velocity, positions, tiles, coefs, counts)
    section = velocity + TIME_STEP * tendency(velocity, inflow, force_a)
    force_b, points_b = forcing(section, positions, tiles, coefs, counts)
    velocity_next = 0.5 * (velocity + section + TIME_STEP * tendency(section, inflow, force_b))
    mean_force = 0.5 * (points_a + points_b)
    blade_force = mean_force.transpose(1, 0, 2)[None]
    return (velocity_next, blade_force)


def solution(mesh):
    return jax.shard_map(
        local,
        mesh=mesh,
        in_specs=(
            P(None, "gx", "gy", None),
            P(None, "gy", None),
            P("gx", None, None, None),
            P("gx", None, None),
            P("gx", None, None),
            P("gx"),
        ),
        out_specs=(P(None, "gx", "gy", None), P("gx", None, None, None)),
        check_vma=False,
    )
```

profile of v0, /device:TPU:1, one launch (start us, length us, event | category | flops | bytes accessed | tf_op | source)
XLA Modules:
  0.0 441.3 jit_solution(17340737165087671309)
XLA Ops:
  7.2 0.9 slice.110
  8.1 0.1 copy.26
  8.2 3.3 collective-permute-start
  11.6 0.8 compare_convert_fusion.1
  12.3 0.9 slice_bitcast_fusion.7
  13.2 0.9 fusion.56
  14.1 15.0 %fusion.61 = f32[64,3,32,256]{3,0,2,1:T(8,128)S(1)} fusion(s32[64]{0:T(128)S(1)} %fusion.56, f32[3,96,32,256]{3,2,1,0:T(8,128)} %param.6), kind=kOutput, calls=%fused_computation.99 | convolution fusion | flops 1811994624 | bytes 15728896 | tf_op jit(solution)/shard_map/ri,cijk->rcjk/dot_general | solution.py:85
  29.1 3.2 select_multiply_fusion
  32.3 27.9 %multiply_reduce_fusion.1 = f32[64,256,3]{1,2,0:T(4,128)S(1)} fusion(f32[64,256,32]{1,2,0:T(8,128)S(1)} %get-tuple-element.25, s32[64,256]{1,0:T(8,128)S(1)} %get-tuple-element.23, f32[64,3,32,256]{3,0,2,1:T(8,128)S(1)} %fusion.61), kind=kOutput, calls=%fused_computation.57 | convolution fusion | flops 4872683520 | bytes 8650752 | tf_op jit(solution)/shard_map/rcjk,rpk->rcjp/dot_general | solution.py:86
  60.2 0.7 copy.91
  61.0 0.5 all-reduce.7.cloned.1.call-start
  61.5 9.1 %copy.38 = f32[3,96,32,256]{3,1,2,0:T(8,128)S(1)} copy(f32[3,96,32,256]{3,2,1,0:T(8,128)} %param.6) | data formatting | bytes 18874368 | tf_op args[0]
  70.6 1.0 fusion.124
  71.6 1.3 collective-permute-start.3
  72.9 1.7 copy-done
  74.5 6.0 %collective-permute-start.2 = (f32[3,96,1,256]{3,1,2,0:T(8,128)}, f32[3,96,1,256]{3,1,2,0:T(8,128)}, u32[]{:S(2)}, u32[]{:S(2)}) collective-permute-start(f32[3,96,1,256]{3,1,2,0:T(8,128)} %get-tuple-element.21), channel_id=1, source_target_pairs={{1,0},{2,1},{3,2},{4,3},{5,4},{6,5},{7,6},{8,7},{9,8},{10,9},{11,1... | collective-permute-start | bytes 884744 | tf_op jit(solution)/shard_map/ppermute | solution.py:26
  80.6 8.2 %slice_bitcast_fusion.5 = (f32[96,32,256]{2,1,0:T(8,128)}, f32[96,32,256]{2,1,0:T(8,128)}, f32[96,32,256]{2,1,0:T(8,128)S(1)}) fusion(f32[3,96,32,256]{3,2,1,0:T(8,128)} %param.6), kind=kLoop, calls=%fused_computation.69 | loop fusion | bytes 18874368 | tf_op jit(solution)/shard_map/mul | solution.py:51
  89.4 5.4 %copy.24 = f32[96,32,256]{2,0,1:T(8,128)} copy(f32[96,32,256]{2,1,0:T(8,128)} %get-tuple-element.15) | data formatting | bytes 6291456 | tf_op jit(solution)/shard_map/mul | solution.py:51
  94.8 5.4 %copy.34 = f32[96,32,256]{2,0,1:T(8,128)} copy(f32[96,32,256]{2,1,0:T(8,128)} %get-tuple-element.16) | data formatting | bytes 6291456 | tf_op jit(solution)/shard_map/mul | solution.py:53
  100.2 3.5 copy.29
  103.7 2.0 fusion.123
  105.7 3.5 collective-permute-start.1
  109.2 36.1 %all-reduce.5.cloned.1.call-done = f32[3,64,256]{2,1,0:T(8,128)} async-done(((f32[3,64,256]{2,1,0:T(8,128)}), f32[3,64,256]{2,1,0:T(8,128)}) %all-reduce.5.cloned.1.call-update) | async-done | bytes 196624 | tf_op jit(solution)/shard_map/psum | solution.py:90
  145.4 0.9 multiply_reduce_fusion.3
  146.3 0.1 fusion.55
  146.4 0.9 broadcast_multiply_fusion.3
  147.4 23.0 %fusion.4 = f32[64,3,32,256]{3,2,1,0:T(8,128)} fusion(s32[64,256]{1,0:T(8,128)} %copy-done.7, f32[3,64,256]{2,1,0:T(8,128)S(1)} %broadcast_multiply_fusion.3, f32[64,32,256]{2,1,0:T(8,128)} %get-tuple-element.24), kind=kOutput, calls=%fused_computation.4 | convolution fusion | flops 4871159808 | bytes 8650752 | tf_op jit(solution)/shard_map/crjp,rpk->rcjk/dot_general | solution.py:93
  170.4 1.0 broadcast_select_fusion.1
  171.4 39.2 %fusion.12 = f32[3,96,32,256]{3,1,2,0:T(8,128)} fusion(f32[3,96,32,256]{3,1,2,0:T(8,128)} %copy-done, f32[3,96,1,256]{3,1,2,0:T(8,128)} %collective-permute-done.2, f32[3,96,1,256]{3,1,2,0:T(8,128)} %collective-permute-done.3, f32[3,1,32,256]{3,1,2,0:T(1,128)} %get-tuple-element.19, f32[3,1,32,256]{3,1,2,0:T(1,128)S(1)} %broadcast_select_fusion.1, ...), kind=kOutput, calls=%fused_computation.28 | convolution fusion | flops 1873336320 | bytes 35389696 | tf_op jit(solution)/shard_map/ri,rcjk->cijk/dot_general | solution.py:94
  210.6 2.0 slice.147
  212.6 1.9 fusion.122
  214.5 8.8 %fusion.58 = f32[64,3,32,256]{3,0,2,1:T(8,128)S(1)} fusion(f32[3,96,32,256]{3,1,2,0:T(8,128)} %fusion.12, s32[64]{0:T(128)S(1)} %fusion.56), kind=kOutput, calls=%fused_computation.96 | convolution fusion | flops 1811994624 | bytes 15728896 | tf_op jit(solution)/shard_map/ri,cijk->rcjk/dot_general | solution.py:85
  223.4 3.6 slice_bitcast_fusion.2
  226.9 2.9 collective-permute-start.4
  229.9 0.9 collective-permute-start.7
  230.8 3.9 collective-permute-start.6
  234.7 28.8 %multiply_reduce_fusion = f32[64,256,3]{1,2,0:T(4,128)S(1)} fusion(f32[64,256,32]{1,2,0:T(8,128)} %copy-done.2, s32[64,256]{1,0:T(8,128)S(1)} %copy-done.8, f32[64,3,32,256]{3,0,2,1:T(8,128)S(1)} %fusion.58), kind=kOutput, calls=%fused_computation.52 | convolution fusion | flops 4872683520 | bytes 8650752 | tf_op jit(solution)/shard_map/rcjk,rpk->rcjp/dot_general | solution.py:86
  263.5 0.7 copy.90
  264.3 2.0 fusion.121
  266.3 4.7 %collective-permute-start.5 = (f32[3,1,32,256]{3,1,2,0:T(1,128)}, f32[3,1,32,256]{3,1,2,0:T(1,128)}, u32[]{:S(2)}, u32[]{:S(2)}) collective-permute-start(f32[3,1,32,256]{3,1,2,0:T(1,128)} %get-tuple-element.11), channel_id=1, source_target_pairs={{0,16},{16,32},{32,48},{48,64},{64,80},{80,96},{96,112},{1,17},{17... | collective-permute-start | bytes 294920 | tf_op jit(solution)/shard_map/ppermute | solution.py:23
  270.9 73.4 %all-reduce.7.cloned.1.call-done = f32[3,64,256]{2,1,0:T(8,128)} async-done(((f32[3,64,256]{2,1,0:T(8,128)}), f32[3,64,256]{2,1,0:T(8,128)}) %all-reduce.7.cloned.1.call-update) | async-done | bytes 196624 | tf_op jit(solution)/shard_map/psum | solution.py:90
  344.4 1.0 multiply_reduce_fusion.2
  345.3 0.9 fusion.54
  346.3 1.6 multiply_bitcast_fusion
  347.9 22.8 %fusion = f32[64,3,32,256]{3,2,1,0:T(8,128)} fusion(s32[64,256]{1,0:T(8,128)} %copy-done.7, f32[3,64,256]{2,1,0:T(8,128)S(1)} %get-tuple-element.7, f32[64,32,256]{2,1,0:T(8,128)} %get-tuple-element.24), kind=kOutput, calls=%fused_computation | convolution fusion | flops 4871159808 | bytes 8650752 | tf_op jit(solution)/shard_map/crjp,rpk->rcjk/dot_general | solution.py:93
  370.7 1.0 broadcast_select_fusion
  371.8 49.6 %fusion.10 = f32[3,96,32,256]{3,1,2,0:T(8,128)} fusion(f32[3,96,32,256]{3,1,2,0:T(8,128)} %fusion.12, f32[3,96,1,256]{3,1,2,0:T(8,128)} %collective-permute-done.6, f32[3,96,1,256]{3,1,2,0:T(8,128)} %collective-permute-done.7, f32[3,1,32,256]{3,1,2,0:T(1,128)S(1)} %copy-done.6, f32[3,1,32,256]{3,1,2,0:T(1,128)S(1)} %broadcast_select_fusion, ...), kind=kOutput, calls=%fused_computation.25 | convolution fusion | flops 1878054912 | bytes 44826880 | tf_op jit(solution)/shard_map/ri,rcjk->cijk/dot_general | solution.py:94
  421.3 12.9 %copy.39 = f32[3,96,32,256]{3,2,1,0:T(8,128)} copy(f32[3,96,32,256]{3,1,2,0:T(8,128)} %fusion.10) | data formatting | bytes 18874368
  (37 shorter events, 0.2 us)
Async XLA Ops:
  7.2 138.2 %all-reduce.5.cloned.1.call-start = ((), (), s32[]{:S(2)}) async-start(), calls=%async_computation | async-start | bytes 393216 | tf_op jit(solution)/shard_map/psum | solution.py:90
  8.2 95.5 %collective-permute-start = (f32[3,1,32,256]{3,1,2,0:T(1,128)S(1)}, f32[3,1,32,256]{3,1,2,0:T(1,128)S(1)}, u32[]{:S(2)}, u32[]{:S(2)}) collective-permute-start(f32[3,1,32,256]{3,1,2,0:T(1,128)S(1)} %copy.26), channel_id=1, source_target_pairs={{16,0},{32,16},{48,32},{64,48},{80,64},{96,80},{112,96},{17,1},{33... | collective-permute-start | bytes 294920 | tf_op jit(solution)/shard_map/ppermute | solution.py:26
  13.2 19.1 %copy-start.7 = (s32[64,256]{1,0:T(8,128)}, s32[64,256]{1,0:T(8,128)S(1)}, u32[]{:S(2)}) copy-start(s32[64,256]{1,0:T(8,128)S(1)} %get-tuple-element.23) | copy-start | bytes 196612
  32.3 27.9 %copy-start.2 = (f32[64,256,32]{1,2,0:T(8,128)}, f32[64,256,32]{1,2,0:T(8,128)S(1)}, u32[]{:S(2)}) copy-start(f32[64,256,32]{1,2,0:T(8,128)S(1)} %get-tuple-element.25) | copy-start | bytes 6291460
  61.0 283.4 %all-reduce.7.cloned.1.call-start = ((), (), s32[]{:S(2)}) async-start(), calls=%async_computation.1 | async-start | bytes 393216 | tf_op jit(solution)/shard_map/psum | solution.py:90
  70.6 3.9 copy-start
  71.6 99.8 %collective-permute-start.3 = (f32[3,96,1,256]{3,1,2,0:T(8,128)}, f32[3,96,1,256]{3,1,2,0:T(8,128)}, u32[]{:S(2)}, u32[]{:S(2)}) collective-permute-start(f32[3,96,1,256]{3,1,2,0:T(8,128)} %get-tuple-element.20), channel_id=1, source_target_pairs={{0,1},{1,2},{2,3},{3,4},{4,5},{5,6},{6,7},{7,8},{8,9},{9,10},{10,1... | collective-permute-start | bytes 884744 | tf_op jit(solution)/shard_map/ppermute | solution.py:23
  74.5 96.8 %collective-permute-start.2 = (f32[3,96,1,256]{3,1,2,0:T(8,128)}, f32[3,96,1,256]{3,1,2,0:T(8,128)}, u32[]{:S(2)}, u32[]{:S(2)}) collective-permute-start(f32[3,96,1,256]{3,1,2,0:T(8,128)} %get-tuple-element.21), channel_id=1, source_target_pairs={{1,0},{2,1},{3,2},{4,3},{5,4},{6,5},{7,6},{8,7},{9,8},{10,9},{11,1... | collective-permute-start | bytes 884744 | tf_op jit(solution)/shard_map/ppermute | solution.py:26
  89.4 56.9 %copy-start.5 = (f32[1,64,256]{2,1,0:T(8,128)S(1)}, f32[1,64,256]{2,1,0:T(8,128)}, u32[]{:S(2)}) copy-start(f32[1,64,256]{2,1,0:T(8,128)} %param.10) | copy-start | bytes 196612
  105.7 64.7 %collective-permute-start.1 = (f32[3,1,32,256]{3,1,2,0:T(1,128)}, f32[3,1,32,256]{3,1,2,0:T(1,128)}, u32[]{:S(2)}, u32[]{:S(2)}) collective-permute-start(f32[3,1,32,256]{3,1,2,0:T(1,128)} %get-tuple-element.18), channel_id=1, source_target_pairs={{0,16},{16,32},{32,48},{48,64},{64,80},{80,96},{96,112},{1,17},{17... | collective-permute-start | bytes 294920 | tf_op jit(solution)/shard_map/ppermute | solution.py:23
  147.4 23.0 %copy-start.4 = (f32[3,32,256]{2,1,0:T(8,128)S(1)}, f32[3,32,256]{2,1,0:T(8,128)}, u32[]{:S(2)}) copy-start(f32[3,32,256]{2,1,0:T(8,128)} %param.7) | copy-start | bytes 294916
  147.4 24.0 %copy-start.1 = (f32[96,32,256]{2,0,1:T(8,128)S(1)}, f32[96,32,256]{2,0,1:T(8,128)}, u32[]{:S(2)}) copy-start(f32[96,32,256]{2,0,1:T(8,128)} %copy.24) | copy-start | bytes 9437188
  210.6 12.7 %slice-start = ((s8[9437184]{0:T(1024)(128)(4,1)}), s8[4194304]{0:T(1024)(128)(4,1)S(1)}, s32[]{:S(2)}) async-start(s8[9437184]{0:T(1024)(128)(4,1)} %bitcast.95), calls=%async_computation.2 | async-start | bytes 8388608
  214.5 8.8 %slice-start.1 = ((s8[9437184]{0:T(1024)(128)(4,1)}), s8[4194304]{0:T(1024)(128)(4,1)S(1)}, s32[]{:S(2)}) async-start(s8[9437184]{0:T(1024)(128)(4,1)} %bitcast.95), calls=%async_computation.3 | async-start | bytes 8388608
  214.5 8.8 %slice-start.2 = ((s8[9437184]{0:T(1024)(128)(4,1)}), s8[1048576]{0:T(1024)(128)(4,1)S(1)}, s32[]{:S(2)}) async-start(s8[9437184]{0:T(1024)(128)(4,1)} %bitcast.95), calls=%async_computation.4 | async-start | bytes 2097152
  223.4 11.4 %copy-start.8 = (s32[64,256]{1,0:T(8,128)S(1)}, s32[64,256]{1,0:T(8,128)}, u32[]{:S(2)}) copy-start(s32[64,256]{1,0:T(8,128)} %copy-done.7) | copy-start | bytes 196612
  226.9 37.4 %collective-permute-start.4 = (f32[3,1,32,256]{3,1,2,0:T(1,128)}, f32[3,1,32,256]{3,1,2,0:T(1,128)}, u32[]{:S(2)}, u32[]{:S(2)}) collective-permute-start(f32[3,1,32,256]{3,1,2,0:T(1,128)} %slice.147), channel_id=1, source_target_pairs={{16,0},{32,16},{48,32},{64,48},{80,64},{96,80},{112,96},{17,1},{33... | collective-permute-start | bytes 294920 | tf_op jit(solution)/shard_map/ppermute | solution.py:26
  229.9 141.9 %collective-permute-start.7 = (f32[3,96,1,256]{3,1,2,0:T(8,128)}, f32[3,96,1,256]{3,1,2,0:T(8,128)}, u32[]{:S(2)}, u32[]{:S(2)}) collective-permute-start(f32[3,96,1,256]{3,1,2,0:T(8,128)} %get-tuple-element.13), channel_id=1, source_target_pairs={{0,1},{1,2},{2,3},{3,4},{4,5},{5,6},{6,7},{7,8},{8,9},{9,10},{10,1... | collective-permute-start | bytes 884744 | tf_op jit(solution)/shard_map/ppermute | solution.py:23
  230.8 115.4 %copy-start.3 = (f32[3,64,256]{2,1,0:T(8,128)S(1)}, f32[3,64,256]{2,1,0:T(8,128)}, u32[]{:S(2)}) copy-start(f32[3,64,256]{2,1,0:T(8,128)} %all-reduce.5.cloned.1.call-done) | copy-start | bytes 589828
  230.8 140.9 %collective-permute-start.6 = (f32[3,96,1,256]{3,1,2,0:T(8,128)}, f32[3,96,1,256]{3,1,2,0:T(8,128)}, u32[]{:S(2)}, u32[]{:S(2)}) collective-permute-start(f32[3,96,1,256]{3,1,2,0:T(8,128)} %get-tuple-element.14), channel_id=1, source_target_pairs={{1,0},{2,1},{3,2},{4,3},{5,4},{6,5},{7,6},{8,7},{9,8},{10,9},{11,1... | collective-permute-start | bytes 884744 | tf_op jit(solution)/shard_map/ppermute | solution.py:26
  266.3 104.5 %collective-permute-start.5 = (f32[3,1,32,256]{3,1,2,0:T(1,128)}, f32[3,1,32,256]{3,1,2,0:T(1,128)}, u32[]{:S(2)}, u32[]{:S(2)}) collective-permute-start(f32[3,1,32,256]{3,1,2,0:T(1,128)} %get-tuple-element.11), channel_id=1, source_target_pairs={{0,16},{16,32},{32,48},{48,64},{64,80},{80,96},{96,112},{1,17},{17... | collective-permute-start | bytes 294920 | tf_op jit(solution)/shard_map/ppermute | solution.py:23
  347.9 23.9 %copy-start.6 = (f32[3,1,32,256]{3,1,2,0:T(1,128)S(1)}, f32[3,1,32,256]{3,1,2,0:T(1,128)}, u32[]{:S(2)}) copy-start(f32[3,1,32,256]{3,1,2,0:T(1,128)} %get-tuple-element.12) | copy-start | bytes 294916
Sparse Core Ops, SparseCore 0:
  61.1 84.2 all-reduce.4
  264.4 79.9 all-reduce.6
where the time goes:
time: 450 us; the launch traced here: 441 us
  matrix products  215 us (48%)
  waiting for transfers between devices  110 us (24%)
  local copies, waits for them, and re-layouts  57.9 us (13%)
  starting transfers between devices  27.2 us (6%)
  other arithmetic  16.3 us (4%)
  between operations  15.2 us (3%)
    psum x2, waiting for transfers between devices, forcing(): sampled = lax.psum(partial_value, 'gy')  110 us
    dot_general x2, matrix products, forcing(): jnp.einsum('ri,rcjk->cijk', along_x, force_slab, precision=highest)  88.8 us
    dot_general x2, matrix products, forcing(): jnp.einsum('rcjk,rpk->rcjp', planes, along_z, precision=highest)  56.6 us
    dot_general x2, matrix products, forcing(): jnp.einsum('crjp,rpk->rcjk', weighted, along_z, precision=highest)  45.8 us
    dot_general x2, matrix products, forcing(): planes = jnp.einsum('ri,cijk->rcjk', along_x, field, precision=highest)  23.7 us
    unnamed x26, local copies, waits for them, and re-layouts  23.7 us
    mul x3, local copies, waits for them, and re-layouts, tendency(): field[0:1] * (east - west) * 0.5 + field[1:2] * (north - south) * 0.5  17.2 us
    ppermute x4, starting transfers between devices, padded(): lax.ppermute(lax.slice_in_dim(block, 0, width, axis=dim), axis, backward)  16.2 us
  transfers between devices with their start and end apart: 10, of which 2 were waited for; matrix products, arithmetic and copies ran while one was open for 38% of the time, Pallas kernels for 0%

commit v1 on v0

v1 whole, which is shorter than its diff:
```python
import functools
import math

import jax
import jax.numpy as jnp
from jax import lax
from jax.experimental import pallas as pl
from jax.experimental.pallas import tpu as pltpu
from jax.sharding import PartitionSpec as P

F32, BF16, I32 = jnp.float32, jnp.bfloat16, jnp.int32
RAD = 2
VISCOSITY = 0.05
TIME_STEP = 0.1
WIDTH_EPS = 1.5
K0, K1, K2 = (
    math.exp(-((d / WIDTH_EPS) ** 2)) / (WIDTH_EPS * math.sqrt(math.pi)) for d in range(3)
)
MESH = pl.DeviceIdType.MESH
VMEM = pl.BlockSpec(memory_space=pltpu.VMEM)
SMEM = pl.BlockSpec(memory_space=pltpu.SMEM)
HBM = pl.BlockSpec(memory_space=pltpu.HBM)
LANES = 128
CHUNKS = 4


def params(**kw):
    return pltpu.CompilerParams(vmem_limit_bytes=16 << 20, **kw)


def local_y(pos_y, tile_y, cells_y, total_y):
    return lax.rem(pos_y - tile_y * cells_y + total_y + total_y // 2, total_y) - total_y // 2


def smooth_z(block):
    near = pltpu.roll(block, 1, 1) + pltpu.roll(block, block.shape[1] - 1, 1)
    far = pltpu.roll(block, 2, 1) + pltpu.roll(block, block.shape[1] - 2, 1)
    return K0 * block + K1 * near + K2 * far


def split_dot(block, pick, dims):
    rows = block.shape[0]
    high = block.astype(BF16)
    low = (block - high.astype(F32)).astype(BF16)
    both = lax.dot_general(
        jnp.concatenate([high, low], axis=0), pick, (dims, ((), ())), preferred_element_type=F32
    )
    return both[:rows] + both[rows:]


def point_pick(pos_ref, rec, depth):
    pos_z = pos_ref[2, pl.ds(rec, 1), :]
    cell = lax.broadcasted_iota(I32, (depth, pos_z.shape[1]), 0)
    return (cell == pos_z).astype(F32).astype(BF16)


def weight_y(pos_ref, rec, tile_y, cells_y, total_y):
    here = local_y(pos_ref[1, pl.ds(rec, 1), :], tile_y, cells_y, total_y)
    dist = jnp.abs(lax.broadcasted_iota(I32, (cells_y, here.shape[1]), 0) - here)
    return jnp.where(
        dist == 0, K0, jnp.where(dist == 1, K1, jnp.where(dist == 2, K2, 0.0))
    ).astype(F32)


def sample_record(field, pos_ref, part_ref, rec, hub, tile_y, total_y):
    comps, _, cells_y, depth = field.shape
    planes = (
        K0 * field[:, hub]
        + K1 * (field[:, hub - 1] + field[:, hub + 1])
        + K2 * (field[:, hub - 2] + field[:, hub + 2])
    )
    smooth = smooth_z(planes.reshape(comps * cells_y, depth))
    inner = split_dot(smooth, point_pick(pos_ref, rec, depth), ((1,), (0,)))
    along = weight_y(pos_ref, rec, tile_y, cells_y, total_y)
    value = jnp.sum(inner.reshape(comps, cells_y, -1) * along[None], axis=1)
    group, row = rec // 8, lax.rem(rec, 8)
    for half in range(2):
        for c in range(comps):
            part_ref[half * 8 + group, c, pl.ds(row, 1), :] = value[
                c : c + 1, half * LANES : (half + 1) * LANES
            ]


def spread_record(field, pos_ref, coef_ref, samp_ref, rec, hub, scale, tile_y, total_y):
    comps, _, cells_y, depth = field.shape
    group, row = rec // 8, lax.rem(rec, 8)
    sampled = [
        jnp.concatenate(
            [samp_ref[half * 8 + group, c, pl.ds(row, 1), :] for half in range(2)], axis=1
        )
        for c in range(comps)
    ]
    speed = jnp.sqrt(sampled[0] * sampled[0] + sampled[1] * sampled[1] + sampled[2] * sampled[2])
    strength = coef_ref[pl.ds(rec, 1), :] * speed * (-scale)
    along = weight_y(pos_ref, rec, tile_y, cells_y, total_y)
    weighted = jnp.concatenate([along * (strength * value) for value in sampled], axis=0)
    slab = split_dot(weighted, point_pick(pos_ref, rec, depth), ((1,), (1,)))
    slab = smooth_z(slab).reshape(comps, cells_y, depth)
    for d, weight in ((-2, K2), (-1, K1), (0, K0), (1, K1), (2, K2)):
        field[:, hub + d] += weight * slab


def sample_first(total_y, groups_y, vel_hbm, pos_ref, tiles_ref, counts_ref,
                 field, part_ref, plan_ref, flags, table, sems):
    recs = pos_ref.shape[1]
    cells_x, cells_y = field.shape[1:3]
    tile_x, tile_y = lax.axis_index("gx"), lax.axis_index("gy")
    load = pltpu.make_async_copy(vel_hbm, field, sems.at[0])
    load.start()
    part_ref[...] = jnp.zeros_like(part_ref)
    here = local_y(pos_ref[1], tile_y, cells_y, total_y)
    near = ((here >= -RAD) & (here < cells_y + RAD)).astype(I32)
    touched = jnp.max(near, axis=1, keepdims=True)
    hub = pos_ref[0, :, 0:LANES] - tile_x * cells_x
    flags[...] = jnp.where(touched > 0, hub, -1)
    fetch = pltpu.make_async_copy(flags, table, sems.at[1])
    fetch.start()
    fetch.wait()

    def place(rec, count):
        hub = table[rec, 0]
        listed = lax.rem(tile_y - tiles_ref[0, rec] + groups_y, groups_y) < tiles_ref[1, rec]
        plan_ref[0, count] = rec
        plan_ref[1, count] = hub
        take = listed & (rec < counts_ref[0]) & (hub >= 0)
        return count + take.astype(I32)

    count = lax.fori_loop(0, recs, place, jnp.int32(0))
    plan_ref[0, LANES - 1] = count
    load.wait()

    @pl.loop(0, count)
    def _(n):
        sample_record(field, pos_ref, part_ref, plan_ref[0, n], plan_ref[1, n], tile_y, total_y)


def spread_and_sample(total_y, plan_ref, pos_ref, coef_ref, samp_ref, _, field, part_ref):
    tile_y = lax.axis_index("gy")
    count = plan_ref[0, LANES - 1]
    part_ref[...] = jnp.zeros_like(part_ref)

    @pl.loop(0, count)
    def _(n):
        spread_record(field, pos_ref, coef_ref, samp_ref, plan_ref[0, n], plan_ref[1, n],
                      TIME_STEP, tile_y, total_y)

    @pl.loop(0, count)
    def _(n):
        sample_record(field, pos_ref, part_ref, plan_ref[0, n], plan_ref[1, n], tile_y, total_y)


def spread_last(total_y, plan_ref, pos_ref, coef_ref, counts_ref, samp_a, samp_b, _,
                field, next_hbm, blade_ref, sems):
    tile_y = lax.axis_index("gy")
    comps, recs, _ = blade_ref.shape
    count = plan_ref[0, LANES - 1]

    @pl.loop(0, count)
    def _(n):
        spread_record(field, pos_ref, coef_ref, samp_b, plan_ref[0, n], plan_ref[1, n],
                      0.5 * TIME_STEP, tile_y, total_y)

    store = pltpu.make_async_copy(field, next_hbm, sems.at[0])
    store.start()
    for half in range(2):
        lanes = pl.ds(half * LANES, LANES)
        for group in range(recs // 8):
            rows = pl.ds(group * 8, 8)
            a = [samp_a[half * 8 + group, c] for c in range(comps)]
            b = [samp_b[half * 8 + group, c] for c in range(comps)]
            speed_a = jnp.sqrt(a[0] * a[0] + a[1] * a[1] + a[2] * a[2])
            speed_b = jnp.sqrt(b[0] * b[0] + b[1] * b[1] + b[2] * b[2])
            rec = group * 8 + lax.broadcasted_iota(I32, (8, LANES), 0)
            strength = jnp.where(rec < counts_ref[0], coef_ref[rows, lanes] * -0.5, 0.0)
            for c in range(comps):
                blade_ref[c, rows, lanes] = strength * (speed_a * a[c] + speed_b * b[c])
    store.wait()


def exchange(groups_x, groups_y, second, *refs):
    if second:
        old, refs = refs[0], refs[1:]
    (field, part_ref, inflow, result, samp_ref,
     y_send, y_recv, x_recv, gathered, mine, send_sem, recv_sem) = refs
    comps, cells_x, cells_y, depth = field.shape
    tile_x, tile_y = lax.axis_index("gx"), lax.axis_index("gy")
    scale = 0.5 if second else 1.0
    last_x = groups_x - 1
    chunk = cells_x // CHUNKS

    def peer(k):
        return lax.rem(tile_y + k, groups_y)

    barrier = pltpu.get_barrier_semaphore()

    @pl.loop(1, groups_y)
    def _(k):
        pl.semaphore_signal(barrier, inc=1, device_id={"gy": peer(k)}, device_id_type=MESH)

    @pl.when(tile_x > 0)
    def _():
        pl.semaphore_signal(barrier, inc=1, device_id={"gx": tile_x - 1}, device_id_type=MESH)

    @pl.when(tile_x < last_x)
    def _():
        pl.semaphore_signal(barrier, inc=1, device_id={"gx": tile_x + 1}, device_id_type=MESH)

    @pl.loop(0, cells_x // 8)
    def _(b):
        rows = pl.ds(b * 8, 8)
        for c in range(comps):
            for half in range(2):
                lanes = pl.ds(half * LANES, LANES)
                y_send[0, half, c, rows, :] = field[c, rows, 0, lanes]
                y_send[1, half, c, rows, :] = field[c, rows, cells_y - 1, lanes]

    @pl.when(tile_x == 0)
    def _():
        x_recv[0] = inflow[...]

    @pl.when(tile_x == last_x)
    def _():
        x_recv[1] = field[:, cells_x - 1]

    neighbours = (tile_x > 0).astype(I32) + (tile_x < last_x).astype(I32)
    pl.semaphore_wait(barrier, groups_y - 1 + neighbours)

    def remote(src, dst, slot, where):
        return pltpu.make_async_remote_copy(
            src_ref=src, dst_ref=dst, send_sem=send_sem.at[slot], recv_sem=recv_sem.at[slot],
            device_id=where, device_id_type=MESH,
        )

    def part_copy(k):
        return remote(part_ref.at[peer(k)], gathered.at[k], k, {"gy": peer(k)})

    def sum_copy(k):
        return remote(mine, samp_ref.at[tile_y], groups_y + k, {"gy": peer(k)})

    def y_copy(q, side):
        rows = pl.ds(q * chunk, chunk)
        return remote(
            y_send.at[1 - side, :, :, rows, :], y_recv.at[side, :, :, rows, :],
            2 * groups_y + 2 * q + side, {"gy": peer(groups_y - 1 if side else 1)},
        )

    x_slot = 2 * groups_y + 2 * CHUNKS
    to_east = remote(field.at[:, cells_x - 1], x_recv.at[0], x_slot, {"gx": tile_x + 1})
    to_west = remote(field.at[:, 0], x_recv.at[1], x_slot + 1, {"gx": tile_x - 1})

    @pl.loop(1, groups_y)
    def _(k):
        part_copy(k).start()

    for q in range(CHUNKS):
        for side in range(2):
            y_copy(q, side).start()

    @pl.when(tile_x < last_x)
    def _():
        to_east.start()

    @pl.when(tile_x > 0)
    def _():
        to_west.start()

    @pl.loop(1, groups_y)
    def _(k):
        part_copy(k).wait_recv()

    total = part_ref[tile_y]
    for k in range(1, groups_y):
        total = total + gathered[k]
    mine[...] = total
    samp_ref[tile_y] = total

    @pl.loop(1, groups_y)
    def _(k):
        sum_copy(k).start()

    row = lax.broadcasted_iota(I32, (cells_y, LANES), 0)
    lane = lax.broadcasted_iota(I32, (cells_y, LANES), 1)
    a = scale * TIME_STEP * VISCOSITY
    b = scale * TIME_STEP * 0.5
    centre = scale * (1.0 - 6.0 * TIME_STEP * VISCOSITY)

    def ghost(side, half, c, i):
        return jnp.concatenate([y_recv[side, half, c, pl.ds(i, 8, stride=0), :]] * (cells_y // 8))

    def plane(i, west, east):
        for half in range(2):
            lanes = pl.ds(half * LANES, LANES)
            others = pl.ds((1 - half) * LANES, LANES)
            bu, bv, bw = (b * field[c, i, :, lanes] for c in range(3))
            for c in range(comps):
                here = field[c, i, :, lanes]
                other = field[c, i, :, others]
                south = jnp.where(row == 0, ghost(0, half, c, i), pltpu.roll(here, 1, 0))
                north = jnp.where(
                    row == cells_y - 1, ghost(1, half, c, i), pltpu.roll(here, cells_y - 1, 0)
                )
                lower = pltpu.roll(here, 1, 1)
                upper = pltpu.roll(here, LANES - 1, 1)
                if half == 0:
                    lower = jnp.where(lane == 0, 0.0, lower)
                    upper = jnp.where(lane == LANES - 1, pltpu.roll(other, LANES - 1, 1), upper)
                else:
                    lower = jnp.where(lane == 0, pltpu.roll(other, 1, 1), lower)
                    upper = jnp.where(lane == LANES - 1, 0.0, upper)
                out = (
                    centre * here
                    + ((a - bu) * east(c, lanes) + (a + bu) * west(c, lanes))
                    + ((a - bv) * north + (a + bv) * south)
                    + ((a - bw) * upper + (a + bw) * lower)
                )
                if second:
                    out = out + 0.5 * old[c, i, :, lanes]
                result[c, i, :, lanes] = out

    for q in range(CHUNKS):
        for side in range(2):
            y_copy(q, side).wait_recv()

        @pl.loop(max(1, q * chunk), min(cells_x - 1, (q + 1) * chunk))
        def _(i):
            plane(
                i,
                lambda c, lanes: field[c, i - 1, :, lanes],
                lambda c, lanes: field[c, i + 1, :, lanes],
            )

    @pl.when(tile_x > 0)
    def _():
        to_east.wait_recv()

    @pl.when(tile_x < last_x)
    def _():
        to_west.wait_recv()

    plane(0, lambda c, lanes: x_recv[0, c, :, lanes], lambda c, lanes: field[c, 1, :, lanes])
    plane(
        cells_x - 1,
        lambda c, lanes: field[c, cells_x - 2, :, lanes],
        lambda c, lanes: x_recv[1, c, :, lanes],
    )

    @pl.loop(1, groups_y)
    def _(k):
        part_copy(k).wait_send()
        sum_copy(k).wait_send()

    for q in range(CHUNKS):
        for side in range(2):
            y_copy(q, side).wait_send()

    @pl.when(tile_x < last_x)
    def _():
        to_east.wait_send()

    @pl.when(tile_x > 0)
    def _():
        to_west.wait_send()

    @pl.loop(1, groups_y)
    def _(k):
        remote(mine, samp_ref.at[peer(groups_y - k)], groups_y + k, {"gy": peer(k)}).wait_recv()


def local(groups_x, groups_y, velocity, inflow, positions, tiles, coefs, counts):
    comps, cells_x, cells_y, depth = velocity.shape
    total_y = cells_y * groups_y
    pos, tiles, coefs = positions[0].transpose(1, 0, 2), tiles[0].T, coefs[0]
    _, recs, points = pos.shape
    velocity = pltpu.with_memory_space_constraint(velocity, pltpu.HBM)
    grid = pltpu.VMEM(velocity.shape, F32)
    table = pltpu.VMEM((groups_y, comps, recs * points // (groups_y * LANES), LANES), F32)
    plan_type = pltpu.SMEM((2, LANES), I32)

    field, part, plan = pl.pallas_call(
        functools.partial(sample_first, total_y, groups_y),
        out_shape=(grid, table, plan_type),
        in_specs=[HBM, VMEM, SMEM, SMEM],
        out_specs=(VMEM, VMEM, SMEM),
        scratch_shapes=[
            pltpu.VMEM((recs, LANES), I32),
            pltpu.SMEM((recs, LANES), I32),
            pltpu.SemaphoreType.DMA((2,)),
        ],
        compiler_params=params(),
        name="sample_first",
    )(velocity, pos, tiles, counts)

    def swap(second, *operands):
        sems = 2 * groups_y + 2 * CHUNKS + 2
        return pl.pallas_call(
            functools.partial(exchange, groups_x, groups_y, second),
            out_shape=(grid, table),
            in_specs=[VMEM] * len(operands),
            out_specs=(VMEM, VMEM),
            scratch_shapes=[
                pltpu.VMEM((2, 2, comps, cells_x, LANES), F32),
                pltpu.VMEM((2, 2, comps, cells_x, LANES), F32),
                pltpu.VMEM((2, comps, cells_y, depth), F32),
                pltpu.VMEM(table.shape, F32),
                pltpu.VMEM(table.shape[1:], F32),
                pltpu.SemaphoreType.DMA((sems,)),
                pltpu.SemaphoreType.DMA((sems,)),
            ],
            compiler_params=params(collective_id=int(second), has_side_effects=True),
            name="exchange_second" if second else "exchange_first",
        )(*operands)

    section, samp_a = swap(False, field, part, inflow)
    section, part = pl.pallas_call(
        functools.partial(spread_and_sample, total_y),
        out_shape=(grid, table),
        in_specs=[SMEM, VMEM, VMEM, VMEM, VMEM],
        out_specs=(VMEM, VMEM),
        input_output_aliases={4: 0},
        compiler_params=params(),
        name="spread_and_sample",
    )(plan, pos, coefs, samp_a, section)
    final, samp_b = swap(True, field, section, part, inflow)
    _, velocity_next, blade = pl.pallas_call(
        functools.partial(spread_last, total_y),
        out_shape=(
            grid,
            jax.ShapeDtypeStruct(velocity.shape, F32),
            jax.ShapeDtypeStruct(pos.shape, F32),
        ),
        in_specs=[SMEM, VMEM, VMEM, SMEM, VMEM, VMEM, VMEM],
        out_specs=(VMEM, HBM, VMEM),
        input_output_aliases={6: 0},
        scratch_shapes=[pltpu.SemaphoreType.DMA((1,))],
        compiler_params=params(),
        name="spread_last",
    )(plan, pos, coefs, counts, samp_a, samp_b, final)
    return (velocity_next, blade.transpose(1, 0, 2)[None])


def solution(mesh):
    return jax.shard_map(
        functools.partial(local, mesh.shape["gx"], mesh.shape["gy"]),
        mesh=mesh,
        in_specs=(
            P(None, "gx", "gy", None),
            P(None, "gy", None),
            P("gx", None, None, None),
            P("gx", None, None),
            P("gx", None, None),
            P("gx"),
        ),
        out_specs=(P(None, "gx", "gy", None), P("gx", None, None, None)),
        check_vma=False,
    )
```

time: 450 us -> 92.9 us (0.21)
  the two profiles are of different devices: /device:TPU:1 before, /device:TPU:49 now
where the time goes in v1:
time: 92.9 us; the launch traced here: 92.7 us
  Pallas kernels  89.8 us (97%)
  local copies, waits for them, and re-layouts  1.61 us (2%)
  between operations  1.34 us (1%)
    pallas_call x2, Pallas kernels, swap(): pl.pallas_call(functools.partial(exchange, groups_x, groups_y, second), o...  46.5 us
    pallas_call x1, Pallas kernels, local(): pl.pallas_call(functools.partial(spread_and_sample, total_y), out_shape=(...  17.3 us
    pallas_call x1, Pallas kernels, local(): pl.pallas_call(functools.partial(spread_last, total_y), out_shape=(grid,...  14 us
    pallas_call x1, Pallas kernels, local(): pl.pallas_call(functools.partial(sample_first, total_y, groups_y), out_sh...  12 us

profile of v1, /device:TPU:49, one launch (start us, length us, event | category | flops | bytes accessed | tf_op | source)
XLA Modules:
  0.0 92.7 jit_solution(5942763300560934980)
XLA Ops:
  1.3 0.0 copy-start
  1.3 0.9 copy-done
  2.2 0.0 copy-start.3
  2.2 0.7 copy-done.3
  2.9 0.0 copy-start.1
  2.9 0.0 copy-start.2
  2.9 12.0 %sample_first.1 = (f32[3,96,32,256]{3,2,1,0:T(8,128)S(1)}, f32[16,3,8,128]{3,2,1,0:T(8,128)S(1)}, s32[2,128]{1,0:T(2,128)S(4)}) custom-call(f32[3,96,32,256]{3,2,1,0:T(8,128)} %vel_hbm.1, s32[3,64,256]{2,1,0:T(8,128)S(1)} %bitcast.10, s32[2,64]{1,0:T(2,128)S(1)} %bitcast.15, s32[1]{0:T(128)S(6)} %copy.12.counts_ref), custom_call_target="tpu_custom_call" | custom-call | tf_op jit(solution)/shard_map/sample_first/pallas_call | solution.py:379
  14.9 0.0 copy-done.1
  14.9 23.3 %exchange_first.1 = (f32[3,96,32,256]{3,2,1,0:T(8,128)S(1)}, f32[16,3,8,128]{3,2,1,0:T(8,128)S(1)}) custom-call(f32[3,96,32,256]{3,2,1,0:T(8,128)S(1)} %get-tuple-element.14.refs_0_, f32[16,3,8,128]{3,2,1,0:T(8,128)S(1)} %get-tuple-element.15.refs_1_, f32[3,32,256]{2,1,0:T(8,128)S(1)} %copy-done.1), custom_call_target="tpu_custom_call" | custom-call | tf_op jit(solution)/shard_map/exchange_first/pallas_call | solution.py:395
  38.2 0.0 copy-done.2
  38.2 17.3 %spread_and_sample.1 = (f32[3,96,32,256]{3,2,1,0:T(8,128)S(1)}, f32[16,3,8,128]{3,2,1,0:T(8,128)S(1)}) custom-call(s32[2,128]{1,0:T(2,128)S(4)} %get-tuple-element.13.plan_ref, s32[3,64,256]{2,1,0:T(8,128)S(1)} %bitcast.11, f32[64,256]{1,0:T(8,128)S(1)} %bitcast.13, ...), custom_call_target="tpu_custom_call", output_to_operand_aliasing={{0}: (4, {})} | custom-call | tf_op jit(solution)/shard_map/spread_and_sample/pallas_call | solution.py:414
  55.6 23.2 %exchange_second.1 = (f32[3,96,32,256]{3,2,1,0:T(8,128)S(1)}, f32[16,3,8,128]{3,2,1,0:T(8,128)S(1)}) custom-call(f32[3,96,32,256]{3,2,1,0:T(8,128)S(1)} %get-tuple-element.14.refs_0_, f32[3,96,32,256]{3,2,1,0:T(8,128)S(1)} %get-tuple-element.18.refs_1_, f32[16,3,8,128]{3,2,1,0:T(8,128)S(1)} %get-tuple-element.19.refs_2_, f32[3,32,256]{2,1,0:T(8,128)S(1)} %copy-done.1), custom_call_target="tpu_custom_call" | custom-call | tf_op jit(solution)/shard_map/exchange_second/pallas_call | solution.py:395
  78.7 14.0 %spread_last.1 = (f32[3,96,32,256]{3,2,1,0:T(8,128)S(1)}, f32[3,96,32,256]{3,2,1,0:T(8,128)}, f32[3,64,256]{2,1,0:T(8,128)}) custom-call(s32[2,128]{1,0:T(2,128)S(4)} %get-tuple-element.13.plan_ref, s32[3,64,256]{2,1,0:T(8,128)S(1)} %bitcast.12, f32[64,256]{1,0:T(8,128)S(1)} %bitcast.14, s32[1]{0:T(128)S(6)} %copy.12.counts_ref, ...), custom_call_target="tpu_custom_call", output_to_operand_aliasing={{0}: (6, {})} | custom-call | tf_op jit(solution)/shard_map/spread_last/pallas_call | solution.py:424
Async XLA Ops:
  1.3 0.9 %copy-start = (s32[1,64,3,256]{3,1,2,0:T(8,128)S(1)}, s32[1,64,3,256]{3,1,2,0:T(8,128)}, u32[]{:S(2)}) copy-start(s32[1,64,3,256]{3,1,2,0:T(8,128)} %param.8) | copy-start | bytes 589828
  2.2 0.7 copy-start.3
  2.9 12.0 %copy-start.1 = (f32[3,32,256]{2,1,0:T(8,128)S(1)}, f32[3,32,256]{2,1,0:T(8,128)}, u32[]{:S(2)}) copy-start(f32[3,32,256]{2,1,0:T(8,128)} %refs_3_.1) | copy-start | bytes 294916
  2.9 35.3 %copy-start.2 = (f32[1,64,256]{2,1,0:T(8,128)S(1)}, f32[1,64,256]{2,1,0:T(8,128)}, u32[]{:S(2)}) copy-start(f32[1,64,256]{2,1,0:T(8,128)} %param.10) | copy-start | bytes 196612

commit v2 on v1

--- a/solution.py
+++ b/solution.py
@@ -21,7 +21,9 @@
 SMEM = pl.BlockSpec(memory_space=pltpu.SMEM)
 HBM = pl.BlockSpec(memory_space=pltpu.HBM)
 LANES = 128
-CHUNKS = 4
+INNER = 4
+STEP = 4
+PIECES = 4
 
 
 def params(**kw):
@@ -180,22 +182,27 @@
 def exchange(groups_x, groups_y, second, *refs):
     if second:
         old, refs = refs[0], refs[1:]
-    (field, part_ref, inflow, result, samp_ref,
-     y_send, y_recv, x_recv, gathered, mine, send_sem, recv_sem) = refs
+    (field, part_ref, inflow, result, samp_ref, y_send, y_recv, x_recv,
+     outer_parts, outer_sums, inner_parts, mine, send_sem, recv_sem) = refs
     comps, cells_x, cells_y, depth = field.shape
     tile_x, tile_y = lax.axis_index("gx"), lax.axis_index("gy")
-    scale = 0.5 if second else 1.0
     last_x = groups_x - 1
-    chunk = cells_x // CHUNKS
-
-    def peer(k):
-        return lax.rem(tile_y + k, groups_y)
+    outer = groups_y // INNER
+    at_outer, at_inner = tile_y // INNER, lax.rem(tile_y, INNER)
+    north, south = lax.rem(tile_y + 1, groups_y), lax.rem(tile_y + groups_y - 1, groups_y)
+
+    def outer_tile(k):
+        return lax.rem(at_outer + k, outer)
+
+    def inner_tile(k):
+        return lax.rem(at_inner + k, INNER)
 
     barrier = pltpu.get_barrier_semaphore()
-
-    @pl.loop(1, groups_y)
-    def _(k):
-        pl.semaphore_signal(barrier, inc=1, device_id={"gy": peer(k)}, device_id_type=MESH)
+    greeted = [outer_tile(k) * INNER + at_inner for k in range(1, outer)]
+    greeted += [at_outer * INNER + inner_tile(k) for k in range(1, INNER)]
+    greeted += [north, south]
+    for where in greeted:
+        pl.semaphore_signal(barrier, inc=1, device_id={"gy": where}, device_id_type=MESH)
 
     @pl.when(tile_x > 0)
     def _():
@@ -206,8 +213,8 @@
         pl.semaphore_signal(barrier, inc=1, device_id={"gx": tile_x + 1}, device_id_type=MESH)
 
     @pl.loop(0, cells_x // 8)
-    def _(b):
-        rows = pl.ds(b * 8, 8)
+    def _(block):
+        rows = pl.ds(block * 8, 8)
         for c in range(comps):
             for half in range(2):
                 lanes = pl.ds(half * LANES, LANES)
@@ -223,7 +230,7 @@
         x_recv[1] = field[:, cells_x - 1]
 
     neighbours = (tile_x > 0).astype(I32) + (tile_x < last_x).astype(I32)
-    pl.semaphore_wait(barrier, groups_y - 1 + neighbours)
+    pl.semaphore_wait(barrier, len(greeted) + neighbours)
 
     def remote(src, dst, slot, where):
         return pltpu.make_async_remote_copy(
@@ -231,30 +238,36 @@
             device_id=where, device_id_type=MESH,
         )
 
-    def part_copy(k):
-        return remote(part_ref.at[peer(k)], gathered.at[k], k, {"gy": peer(k)})
-
-    def sum_copy(k):
-        return remote(mine, samp_ref.at[tile_y], groups_y + k, {"gy": peer(k)})
-
-    def y_copy(q, side):
-        rows = pl.ds(q * chunk, chunk)
-        return remote(
-            y_send.at[1 - side, :, :, rows, :], y_recv.at[side, :, :, rows, :],
-            2 * groups_y + 2 * q + side, {"gy": peer(groups_y - 1 if side else 1)},
-        )
-
-    x_slot = 2 * groups_y + 2 * CHUNKS
-    to_east = remote(field.at[:, cells_x - 1], x_recv.at[0], x_slot, {"gx": tile_x + 1})
-    to_west = remote(field.at[:, 0], x_recv.at[1], x_slot + 1, {"gx": tile_x - 1})
-
-    @pl.loop(1, groups_y)
-    def _(k):
-        part_copy(k).start()
-
-    for q in range(CHUNKS):
-        for side in range(2):
-            y_copy(q, side).start()
+    def scatter_outer(k):
+        there = outer_tile(k)
+        return remote(part_ref.at[pl.ds(there * INNER, INNER)], outer_parts.at[k - 1], k - 1,
+                      {"gy": there * INNER + at_inner})
+
+    def scatter_inner(k):
+        there = inner_tile(k)
+        return remote(outer_sums.at[there], inner_parts.at[k - 1], outer + k - 2,
+                      {"gy": at_outer * INNER + there})
+
+    base = outer + INNER - 2
+
+    def gather_inner(k, from_tile):
+        return remote(mine, samp_ref.at[from_tile], base + k - 1,
+                      {"gy": at_outer * INNER + inner_tile(k)})
+
+    def gather_outer(k, from_outer):
+        block = pl.ds(from_outer * INNER, INNER)
+        return remote(samp_ref.at[pl.ds(at_outer * INNER, INNER)], samp_ref.at[block],
+                      base + INNER + k - 2, {"gy": outer_tile(k) * INNER + at_inner})
+
+    to_north = remote(y_send.at[1], y_recv.at[0], 2 * base, {"gy": north})
+    to_south = remote(y_send.at[0], y_recv.at[1], 2 * base + 1, {"gy": south})
+    to_east = remote(field.at[:, cells_x - 1], x_recv.at[0], 2 * base + 2, {"gx": tile_x + 1})
+    to_west = remote(field.at[:, 0], x_recv.at[1], 2 * base + 3, {"gx": tile_x - 1})
+
+    for k in range(1, outer):
+        scatter_outer(k).start()
+    to_north.start()
+    to_south.start()
 
     @pl.when(tile_x < last_x)
     def _():
@@ -264,70 +277,101 @@
     def _():
         to_west.start()
 
-    @pl.loop(1, groups_y)
-    def _(k):
-        part_copy(k).wait_recv()
-
-    total = part_ref[tile_y]
-    for k in range(1, groups_y):
-        total = total + gathered[k]
-    mine[...] = total
-    samp_ref[tile_y] = total
-
-    @pl.loop(1, groups_y)
-    def _(k):
-        sum_copy(k).start()
-
-    row = lax.broadcasted_iota(I32, (cells_y, LANES), 0)
-    lane = lax.broadcasted_iota(I32, (cells_y, LANES), 1)
+    scale = 0.5 if second else 1.0
     a = scale * TIME_STEP * VISCOSITY
     b = scale * TIME_STEP * 0.5
     centre = scale * (1.0 - 6.0 * TIME_STEP * VISCOSITY)
+    sub = lax.broadcasted_iota(I32, (8, LANES), 0)
+    lane = lax.broadcasted_iota(I32, (8, LANES), 1)
+    first_row, last_row = sub == 0, sub == 7
+    first_lane, last_lane = lane == 0, lane == LANES - 1
+    zero = jnp.zeros((8, LANES), F32)
+    halves = [pl.ds(half * LANES, LANES) for half in range(2)]
+    strips = cells_y // 8
+
+    def tile(c, i, t, half):
+        return field[c, i, pl.ds(8 * t, 8), halves[half]]
 
     def ghost(side, half, c, i):
-        return jnp.concatenate([y_recv[side, half, c, pl.ds(i, 8, stride=0), :]] * (cells_y // 8))
-
-    def plane(i, west, east):
-        for half in range(2):
-            lanes = pl.ds(half * LANES, LANES)
-            others = pl.ds((1 - half) * LANES, LANES)
-            bu, bv, bw = (b * field[c, i, :, lanes] for c in range(3))
+        return y_recv[side, half, c, pl.ds(i, 8, stride=0), :]
+
+    def plane(i, west, east, ghosts):
+        for t in range(strips):
+            rows = pl.ds(8 * t, 8)
+            here = [[tile(c, i, t, half) for half in range(2)] for c in range(comps)]
+            lower, upper = [], []
             for c in range(comps):
-                here = field[c, i, :, lanes]
-                other = field[c, i, :, others]
-                south = jnp.where(row == 0, ghost(0, half, c, i), pltpu.roll(here, 1, 0))
-                north = jnp.where(
-                    row == cells_y - 1, ghost(1, half, c, i), pltpu.roll(here, cells_y - 1, 0)
-                )
-                lower = pltpu.roll(here, 1, 1)
-                upper = pltpu.roll(here, LANES - 1, 1)
-                if half == 0:
-                    lower = jnp.where(lane == 0, 0.0, lower)
-                    upper = jnp.where(lane == LANES - 1, pltpu.roll(other, LANES - 1, 1), upper)
-                else:
-                    lower = jnp.where(lane == 0, pltpu.roll(other, 1, 1), lower)
-                    upper = jnp.where(lane == LANES - 1, 0.0, upper)
-                out = (
-                    centre * here
-                    + ((a - bu) * east(c, lanes) + (a + bu) * west(c, lanes))
-                    + ((a - bv) * north + (a + bv) * south)
-                    + ((a - bw) * upper + (a + bw) * lower)
-                )
-                if second:
-                    out = out + 0.5 * old[c, i, :, lanes]
-                result[c, i, :, lanes] = out
-
-    for q in range(CHUNKS):
-        for side in range(2):
-            y_copy(q, side).wait_recv()
-
-        @pl.loop(max(1, q * chunk), min(cells_x - 1, (q + 1) * chunk))
-        def _(i):
-            plane(
-                i,
-                lambda c, lanes: field[c, i - 1, :, lanes],
-                lambda c, lanes: field[c, i + 1, :, lanes],
-            )
+                up = [pltpu.roll(v, 1, 1) for v in here[c]]
+                down = [pltpu.roll(v, LANES - 1, 1) for v in here[c]]
+                lower.append([jnp.where(first_lane, zero, up[0]), jnp.where(first_lane, up[0], up[1])])
+                upper.append([jnp.where(last_lane, down[1], down[0]), jnp.where(last_lane, zero, down[1])])
+            for half in range(2):
+                bu, bv, bw = (b * here[c][half] for c in range(3))
+                for c in range(comps):
+                    if t > 0:
+                        below = pltpu.roll(tile(c, i, t - 1, half), 1, 0)
+                    else:
+                        below = ghost(0, half, c, i) if ghosts else zero
+                    if t < strips - 1:
+                        above = pltpu.roll(tile(c, i, t + 1, half), 7, 0)
+                    else:
+                        above = ghost(1, half, c, i) if ghosts else zero
+                    value = here[c][half]
+                    to_s = jnp.where(first_row, below, pltpu.roll(value, 1, 0))
+                    to_n = jnp.where(last_row, above, pltpu.roll(value, 7, 0))
+                    out = (
+                        centre * value
+                        + ((a - bu) * east(c, rows, halves[half]) + (a + bu) * west(c, rows, halves[half]))
+                        + ((a - bv) * to_n + (a + bv) * to_s)
+                        + ((a - bw) * upper[c][half] + (a + bw) * lower[c][half])
+                    )
+                    if second:
+                        out = out + 0.5 * old[c, i, rows, halves[half]]
+                    result[c, i, rows, halves[half]] = out
+
+    def inside(i, ghosts):
+        plane(
+            i,
+            lambda c, rows, lanes: field[c, i - 1, rows, lanes],
+            lambda c, rows, lanes: field[c, i + 1, rows, lanes],
+            ghosts,
+        )
+
+    def piece(start, stop, ghosts):
+        @pl.loop(0, (stop - start) // STEP)
+        def _(n):
+            for k in range(STEP):
+                inside(start + n * STEP + k, ghosts)
+
+    steps = (cells_x - 2) // STEP
+    cuts = [1 + STEP * (steps * k // PIECES) for k in range(PIECES + 1)]
+
+    piece(cuts[0], cuts[1], False)
+    for k in range(1, outer):
+        scatter_outer(k).wait_recv()
+    outer_sums[...] = functools.reduce(
+        jnp.add, [outer_parts[k] for k in range(outer - 1)], part_ref[pl.ds(at_outer * INNER, INNER)]
+    )
+    for k in range(1, INNER):
+        scatter_inner(k).start()
+    piece(cuts[1], cuts[2], False)
+    for k in range(1, INNER):
+        scatter_inner(k).wait_recv()
+    total = functools.reduce(jnp.add, [inner_parts[k] for k in range(INNER - 1)], outer_sums[at_inner])
+    mine[...] = total
+    samp_ref[tile_y] = total
+    for k in range(1, INNER):
+        gather_inner(k, tile_y).start()
+    piece(cuts[2], cuts[3], False)
+    for k in range(1, INNER):
+        gather_inner(k, at_outer * INNER + inner_tile(INNER - k)).wait_recv()
+    for k in range(1, outer):
+        gather_outer(k, at_outer).start()
+    to_north.wait_recv()
+    to_south.wait_recv()
+    piece(cuts[3], cuts[4], True)
+    for i in range(cuts[4], cells_x - 1):
+        inside(i, True)
 
     @pl.when(tile_x > 0)
     def _():
@@ -337,21 +381,42 @@
     def _():
         to_west.wait_recv()
 
-    plane(0, lambda c, lanes: x_recv[0, c, :, lanes], lambda c, lanes: field[c, 1, :, lanes])
+    plane(
+        0,
+        lambda c, rows, lanes: x_recv[0, c, rows, lanes],
+        lambda c, rows, lanes: field[c, 1, rows, lanes],
+        True,
+    )
     plane(
         cells_x - 1,
-        lambda c, lanes: field[c, cells_x - 2, :, lanes],
-        lambda c, lanes: x_recv[1, c, :, lanes],
+        lambda c, rows, lanes: field[c, cells_x - 2, rows, lanes],
+        lambda c, rows, lanes: x_recv[1, c, rows, lanes],
+        True,
     )
 
-    @pl.loop(1, groups_y)
-    def _(k):
-        part_copy(k).wait_send()
-        sum_copy(k).wait_send()
-
-    for q in range(CHUNKS):
-        for side in range(2):
-            y_copy(q, side).wait_send()
+    @pl.loop(0, (cuts[3] - cuts[0]) // STEP)
+    def _(n):
+        for k in range(STEP):
+            i = cuts[0] + n * STEP + k
+            for side, t, mask in ((0, 0, first_row), (1, strips - 1, last_row)):
+                rows = pl.ds(8 * t, 8)
+                for half in range(2):
+                    bv = b * tile(1, i, t, half)
+                    weight = jnp.where(mask, a - bv if side else a + bv, 0.0)
+                    for c in range(comps):
+                        before = result[c, i, rows, halves[half]]
+                        result[c, i, rows, halves[half]] = before + weight * ghost(side, half, c, i)
+
+    for k in range(1, outer):
+        gather_outer(k, outer_tile(outer - k)).wait_recv()
+    for k in range(1, outer):
+        scatter_outer(k).wait_send()
+        gather_outer(k, at_outer).wait_send()
+    for k in range(1, INNER):
+        scatter_inner(k).wait_send()
+        gather_inner(k, tile_y).wait_send()
+    to_north.wait_send()
+    to_south.wait_send()
 
     @pl.when(tile_x < last_x)
     def _():
@@ -360,10 +425,6 @@
     @pl.when(tile_x > 0)
     def _():
         to_west.wait_send()
-
-    @pl.loop(1, groups_y)
-    def _(k):
-        remote(mine, samp_ref.at[peer(groups_y - k)], groups_y + k, {"gy": peer(k)}).wait_recv()
 
 
 def local(groups_x, groups_y, velocity, inflow, positions, tiles, coefs, counts):
@@ -391,7 +452,8 @@
     )(velocity, pos, tiles, counts)
 
     def swap(second, *operands):
-        sems = 2 * groups_y + 2 * CHUNKS + 2
+        outer = groups_y // INNER
+        sems = 2 * (outer + INNER - 2) + 4
         return pl.pallas_call(
             functools.partial(exchange, groups_x, groups_y, second),
             out_shape=(grid, table),
@@ -401,7 +463,9 @@
                 pltpu.VMEM((2, 2, comps, cells_x, LANES), F32),
                 pltpu.VMEM((2, 2, comps, cells_x, LANES), F32),
                 pltpu.VMEM((2, comps, cells_y, depth), F32),
-                pltpu.VMEM(table.shape, F32),
+                pltpu.VMEM((outer - 1, INNER, *table.shape[1:]), F32),
+                pltpu.VMEM((INNER, *table.shape[1:]), F32),
+                pltpu.VMEM((INNER - 1, *table.shape[1:]), F32),
                 pltpu.VMEM(table.shape[1:], F32),
                 pltpu.SemaphoreType.DMA((sems,)),
                 pltpu.SemaphoreType.DMA((sems,)),

time: 92.9 us -> 85.5 us (0.920)
  the two profiles are of different devices: /device:TPU:49 before, /device:TPU:65 now
where the time goes in v2:
time: 85.5 us; the launch traced here: 85.3 us
  Pallas kernels  82.4 us (96%)
  local copies, waits for them, and re-layouts  1.61 us (2%)
  between operations  1.34 us (2%)
    pallas_call x2, Pallas kernels, swap(): pl.pallas_call(functools.partial(exchange, groups_x, groups_y, second), o...  36.3 us
    pallas_call x1, Pallas kernels, local(): pl.pallas_call(functools.partial(spread_and_sample, total_y), out_shape=(...  18.7 us
    pallas_call x1, Pallas kernels, local(): pl.pallas_call(functools.partial(spread_last, total_y), out_shape=(grid,...  14.7 us
    pallas_call x1, Pallas kernels, local(): pl.pallas_call(functools.partial(sample_first, total_y, groups_y), out_sh...  12.6 us

profile of v2, /device:TPU:65, one launch (start us, length us, event | category | flops | bytes accessed | tf_op | source)
XLA Modules:
  0.0 85.3 jit_solution(1470592450579205301)
XLA Ops:
  1.3 0.0 copy-start
  1.3 0.9 %copy-done = s32[1,64,3,256]{3,1,2,0:T(8,128)S(1)} copy-done((s32[1,64,3,256]{3,1,2,0:T(8,128)S(1)}, s32[1,64,3,256]{3,1,2,0:T(8,128)}, u32[]{:S(2)}) %copy-start) | copy-done | bytes 196632
  2.2 0.0 copy-start.3
  2.2 0.7 copy-done.3
  2.9 0.0 copy-start.1
  2.9 0.0 copy-start.2
  2.9 12.6 %sample_first.1 = (f32[3,96,32,256]{3,2,1,0:T(8,128)S(1)}, f32[16,3,8,128]{3,2,1,0:T(8,128)S(1)}, s32[2,128]{1,0:T(2,128)S(4)}) custom-call(f32[3,96,32,256]{3,2,1,0:T(8,128)} %vel_hbm.1, s32[3,64,256]{2,1,0:T(8,128)S(1)} %bitcast.10, s32[2,64]{1,0:T(2,128)S(1)} %bitcast.15, s32[1]{0:T(128)S(6)} %copy.12.counts_ref), custom_call_target="tpu_custom_call" | custom-call | tf_op jit(solution)/shard_map/sample_first/pallas_call | solution.py:440
  15.5 0.0 copy-done.1
  15.5 18.5 %exchange_first.1 = (f32[3,96,32,256]{3,2,1,0:T(8,128)S(1)}, f32[16,3,8,128]{3,2,1,0:T(8,128)S(1)}) custom-call(f32[3,96,32,256]{3,2,1,0:T(8,128)S(1)} %get-tuple-element.14.refs_0_, f32[16,3,8,128]{3,2,1,0:T(8,128)S(1)} %get-tuple-element.15.refs_1_, f32[3,32,256]{2,1,0:T(8,128)S(1)} %copy-done.1), custom_call_target="tpu_custom_call" | custom-call | tf_op jit(solution)/shard_map/exchange_first/pallas_call | solution.py:457
  34.0 0.0 copy-done.2
  34.0 18.7 %spread_and_sample.1 = (f32[3,96,32,256]{3,2,1,0:T(8,128)S(1)}, f32[16,3,8,128]{3,2,1,0:T(8,128)S(1)}) custom-call(s32[2,128]{1,0:T(2,128)S(4)} %get-tuple-element.13.plan_ref, s32[3,64,256]{2,1,0:T(8,128)S(1)} %bitcast.11, f32[64,256]{1,0:T(8,128)S(1)} %bitcast.13, ...), custom_call_target="tpu_custom_call", output_to_operand_aliasing={{0}: (4, {})} | custom-call | tf_op jit(solution)/shard_map/spread_and_sample/pallas_call | solution.py:478
  52.7 17.8 %exchange_second.1 = (f32[3,96,32,256]{3,2,1,0:T(8,128)S(1)}, f32[16,3,8,128]{3,2,1,0:T(8,128)S(1)}) custom-call(f32[3,96,32,256]{3,2,1,0:T(8,128)S(1)} %get-tuple-element.14.refs_0_, f32[3,96,32,256]{3,2,1,0:T(8,128)S(1)} %get-tuple-element.18.refs_1_, f32[16,3,8,128]{3,2,1,0:T(8,128)S(1)} %get-tuple-element.19.refs_2_, f32[3,32,256]{2,1,0:T(8,128)S(1)} %copy-done.1), custom_call_target="tpu_custom_call" | custom-call | tf_op jit(solution)/shard_map/exchange_second/pallas_call | solution.py:457
  70.6 14.7 %spread_last.1 = (f32[3,96,32,256]{3,2,1,0:T(8,128)S(1)}, f32[3,96,32,256]{3,2,1,0:T(8,128)}, f32[3,64,256]{2,1,0:T(8,128)}) custom-call(s32[2,128]{1,0:T(2,128)S(4)} %get-tuple-element.13.plan_ref, s32[3,64,256]{2,1,0:T(8,128)S(1)} %bitcast.12, f32[64,256]{1,0:T(8,128)S(1)} %bitcast.14, s32[1]{0:T(128)S(6)} %copy.12.counts_ref, ...), custom_call_target="tpu_custom_call", output_to_operand_aliasing={{0}: (6, {})} | custom-call | tf_op jit(solution)/shard_map/spread_last/pallas_call | solution.py:488
Async XLA Ops:
  1.3 0.9 %copy-start = (s32[1,64,3,256]{3,1,2,0:T(8,128)S(1)}, s32[1,64,3,256]{3,1,2,0:T(8,128)}, u32[]{:S(2)}) copy-start(s32[1,64,3,256]{3,1,2,0:T(8,128)} %param.8) | copy-start | bytes 589828
  2.2 0.7 copy-start.3
  2.9 12.6 %copy-start.1 = (f32[3,32,256]{2,1,0:T(8,128)S(1)}, f32[3,32,256]{2,1,0:T(8,128)}, u32[]{:S(2)}) copy-start(f32[3,32,256]{2,1,0:T(8,128)} %refs_3_.1) | copy-start | bytes 294916
  2.9 31.1 %copy-start.2 = (f32[1,64,256]{2,1,0:T(8,128)S(1)}, f32[1,64,256]{2,1,0:T(8,128)}, u32[]{:S(2)}) copy-start(f32[1,64,256]{2,1,0:T(8,128)} %param.10) | copy-start | bytes 196612

commit v3 on v2

v3 whole, which is shorter than its diff:
```python
import functools
import math

import jax
import jax.numpy as jnp
from jax import lax
from jax.experimental import pallas as pl
from jax.experimental.pallas import tpu as pltpu
from jax.sharding import PartitionSpec as P

F32, BF16, I32 = jnp.float32, jnp.bfloat16, jnp.int32
RAD = 2
VISCOSITY = 0.05
TIME_STEP = 0.1
WIDTH_EPS = 1.5
K0, K1, K2 = (
    math.exp(-((d / WIDTH_EPS) ** 2)) / (WIDTH_EPS * math.sqrt(math.pi)) for d in range(3)
)
MESH = pl.DeviceIdType.MESH
VMEM = pl.BlockSpec(memory_space=pltpu.VMEM)
SMEM = pl.BlockSpec(memory_space=pltpu.SMEM)
HBM = pl.BlockSpec(memory_space=pltpu.HBM)
LANES = 128
STEP = 4
CHUNKS = 4


def params(**kw):
    return pltpu.CompilerParams(vmem_limit_bytes=16 << 20, **kw)


def local_y(pos_y, tile_y, cells_y, total_y):
    return lax.rem(pos_y - tile_y * cells_y + total_y + total_y // 2, total_y) - total_y // 2


def smooth_z(block):
    near = pltpu.roll(block, 1, 1) + pltpu.roll(block, block.shape[1] - 1, 1)
    far = pltpu.roll(block, 2, 1) + pltpu.roll(block, block.shape[1] - 2, 1)
    return K0 * block + K1 * near + K2 * far


def split_dot(block, pick, dims):
    rows = block.shape[0]
    high = block.astype(BF16)
    low = (block - high.astype(F32)).astype(BF16)
    both = lax.dot_general(
        jnp.concatenate([high, low], axis=0), pick, (dims, ((), ())), preferred_element_type=F32
    )
    return both[:rows] + both[rows:]


def build_tables(pos_ref, pick_ref, along_ref, n, rec, tile_y, total_y):
    depth, points = pick_ref.shape[1:]
    cells_y = along_ref.shape[1]
    cell = lax.broadcasted_iota(I32, (depth, points), 0)
    pick_ref[n] = (cell == pos_ref[2, pl.ds(rec, 1), :]).astype(F32).astype(BF16)
    here = local_y(pos_ref[1, pl.ds(rec, 1), :], tile_y, cells_y, total_y)
    dist = jnp.abs(lax.broadcasted_iota(I32, (cells_y, points), 0) - here)
    along_ref[n] = jnp.where(
        dist == 0, K0, jnp.where(dist == 1, K1, jnp.where(dist == 2, K2, 0.0))
    ).astype(F32)


def sample_pair(field, plan_ref, pick_ref, along_ref, part_ref, pair, count):
    comps, _, cells_y, depth = field.shape
    for n in (2 * pair, jnp.minimum(2 * pair + 1, count - 1)):
        rec, hub = plan_ref[0, n], plan_ref[1, n]
        planes = (
            K0 * field[:, hub]
            + K1 * (field[:, hub - 1] + field[:, hub + 1])
            + K2 * (field[:, hub - 2] + field[:, hub + 2])
        )
        smooth = smooth_z(planes.reshape(comps * cells_y, depth))
        inner = split_dot(smooth, pick_ref[n], ((1,), (0,)))
        value = jnp.sum(inner.reshape(comps, cells_y, -1) * along_ref[n][None], axis=1)
        group, row = rec // 8, lax.rem(rec, 8)
        for half in range(2):
            for c in range(comps):
                part_ref[half * 8 + group, c, pl.ds(row, 1), :] = value[
                    c : c + 1, half * LANES : (half + 1) * LANES
                ]


def spread_pair(field, plan_ref, pick_ref, along_ref, coef_ref, samp_ref, scale, pair, count):
    comps, _, cells_y, depth = field.shape
    slabs = []
    for k in range(2):
        n = jnp.minimum(2 * pair + k, count - 1)
        rec, hub = plan_ref[0, n], plan_ref[1, n]
        factor = jnp.where(2 * pair + k < count, -scale, 0.0)
        group, row = rec // 8, lax.rem(rec, 8)
        sampled = [
            jnp.concatenate(
                [samp_ref[half * 8 + group, c, pl.ds(row, 1), :] for half in range(2)], axis=1
            )
            for c in range(comps)
        ]
        speed = jnp.sqrt(sampled[0] * sampled[0] + sampled[1] * sampled[1] + sampled[2] * sampled[2])
        strength = coef_ref[pl.ds(rec, 1), :] * speed * factor
        along = along_ref[n]
        weighted = jnp.concatenate([along * (strength * value) for value in sampled], axis=0)
        slab = smooth_z(split_dot(weighted, pick_ref[n], ((1,), (1,))))
        slabs.append((hub, slab.reshape(comps, cells_y, depth)))
    for hub, slab in slabs:
        for d, weight in ((-2, K2), (-1, K1), (0, K0), (1, K1), (2, K2)):
            field[:, hub + d] += weight * slab


def make_plan(total_y, groups_y, pos_ref, tiles_ref, counts_ref, rows_ref, cells_x, cells_y):
    recs = pos_ref.shape[1]
    tile_x, tile_y = lax.axis_index("gx"), lax.axis_index("gy")
    rec = lax.broadcasted_iota(I32, (recs, LANES), 0)
    lane = lax.broadcasted_iota(I32, (recs, LANES), 1)
    square = lax.broadcasted_iota(I32, (recs, recs), 0) == lax.broadcasted_iota(I32, (recs, recs), 1)

    def column(row):
        return jnp.sum(jnp.where(square, row.astype(F32), 0.0), axis=1, keepdims=True).astype(I32)

    here = local_y(pos_ref[1], tile_y, cells_y, total_y)
    near = ((here >= -RAD) & (here < cells_y + RAD)).astype(I32)
    touched = jnp.max(near, axis=1, keepdims=True)
    hub = pos_ref[0, :, 0:1] - tile_x * cells_x
    first, number = column(tiles_ref[0:1, :]), column(tiles_ref[1:2, :])
    listed = lax.rem(tile_y - first + groups_y, groups_y) < number
    active = listed & (touched > 0) & (rec[:, 0:1] < counts_ref[0])
    big = jnp.int32(1 << 20)
    key = jnp.where(active, hub * recs + rec[:, 0:1], big)
    key_row = jnp.min(jnp.where(rec == lane, key, big), axis=0, keepdims=True)
    rank = jnp.sum((key_row < key).astype(F32), axis=1, keepdims=True).astype(I32)
    live = active.astype(F32)
    count = jnp.sum(live, axis=0, keepdims=True).astype(I32)
    mine = active & (rank == jnp.minimum(lane, count - 1))
    rows_ref[0:1, :] = jnp.sum(jnp.where(mine, rec, 0).astype(F32), axis=0, keepdims=True).astype(I32)
    rows_ref[1:2, :] = jnp.sum(jnp.where(mine, hub, 0).astype(F32), axis=0, keepdims=True).astype(I32)
    below = active & (hub < lane)
    rows_ref[2:3, :] = jnp.sum(below.astype(F32), axis=0, keepdims=True).astype(I32)


def sample_first(total_y, groups_y, vel_hbm, pos_hbm, tiles_hbm, counts_ref,
                 field, pos_ref, part_ref, plan_ref, pick_ref, along_ref, tiles_ref, rows_ref, sems):
    cells_x, cells_y = field.shape[1:3]
    tile_y = lax.axis_index("gy")
    chunk = cells_x // CHUNKS
    fetch_pos = pltpu.make_async_copy(pos_hbm, pos_ref, sems.at[CHUNKS])
    fetch_tiles = pltpu.make_async_copy(tiles_hbm, tiles_ref, sems.at[CHUNKS + 1])
    fetch_pos.start()
    fetch_tiles.start()
    loads = []
    for q in range(CHUNKS):
        planes = pl.ds(q * chunk, chunk)
        loads.append(pltpu.make_async_copy(vel_hbm.at[:, planes], field.at[:, planes], sems.at[q]))
        loads[-1].start()
    part_ref[...] = jnp.zeros_like(part_ref)
    rows_ref[...] = jnp.zeros_like(rows_ref)
    fetch_pos.wait()
    fetch_tiles.wait()
    make_plan(total_y, groups_y, pos_ref, tiles_ref, counts_ref, rows_ref, cells_x, cells_y)
    fetch_plan = pltpu.make_async_copy(rows_ref, plan_ref, sems.at[CHUNKS + 2])
    fetch_plan.start()
    fetch_plan.wait()
    count = plan_ref[2, LANES - 1]

    @pl.loop(0, count)
    def _(n):
        build_tables(pos_ref, pick_ref, along_ref, n, plan_ref[0, n], tile_y, total_y)

    start = jnp.int32(0)
    for q in range(CHUNKS):
        loads[q].wait()
        if q < CHUNKS - 1:
            stop = plan_ref[2, (q + 1) * chunk - RAD] // 2
        else:
            stop = (count + 1) // 2

        @pl.loop(start, stop)
        def _(pair):
            sample_pair(field, plan_ref, pick_ref, along_ref, part_ref, pair, count)

        start = stop


def spread_and_sample(plan_ref, pick_ref, along_ref, coef_ref, samp_ref, _, field, part_ref):
    count = plan_ref[2, LANES - 1]
    part_ref[...] = jnp.zeros_like(part_ref)

    @pl.loop(0, (count + 1) // 2)
    def _(pair):
        spread_pair(field, plan_ref, pick_ref, along_ref, coef_ref, samp_ref, TIME_STEP, pair, count)

    @pl.loop(0, (count + 1) // 2)
    def _(pair):
        sample_pair(field, plan_ref, pick_ref, along_ref, part_ref, pair, count)


def spread_last(plan_ref, pick_ref, along_ref, coef_ref, counts_ref, samp_a, samp_b, _,
                field, next_hbm, blade_ref, sems):
    comps, recs, _ = blade_ref.shape
    chunk = field.shape[1] // CHUNKS
    count = plan_ref[2, LANES - 1]
    start = jnp.int32(0)
    stores = []
    for q in range(CHUNKS):
        if q < CHUNKS - 1:
            stop = (plan_ref[2, (q + 1) * chunk + RAD] + 1) // 2
        else:
            stop = (count + 1) // 2

        @pl.loop(start, stop)
        def _(pair):
            spread_pair(field, plan_ref, pick_ref, along_ref, coef_ref, samp_b,
                        0.5 * TIME_STEP, pair, count)

        planes = pl.ds(q * chunk, chunk)
        stores.append(pltpu.make_async_copy(field.at[:, planes], next_hbm.at[:, planes], sems.at[q]))
        stores[-1].start()
        start = stop

    for half in range(2):
        lanes = pl.ds(half * LANES, LANES)
        for group in range(recs // 8):
            rows = pl.ds(group * 8, 8)
            a = [samp_a[half * 8 + group, c] for c in range(comps)]
            b = [samp_b[half * 8 + group, c] for c in range(comps)]
            speed_a = jnp.sqrt(a[0] * a[0] + a[1] * a[1] + a[2] * a[2])
            speed_b = jnp.sqrt(b[0] * b[0] + b[1] * b[1] + b[2] * b[2])
            rec = group * 8 + lax.broadcasted_iota(I32, (8, LANES), 0)
            strength = jnp.where(rec < counts_ref[0], coef_ref[rows, lanes] * -0.5, 0.0)
            for c in range(comps):
                blade_ref[c, rows, lanes] = strength * (speed_a * a[c] + speed_b * b[c])
    for store in stores:
        store.wait()


def exchange(groups_x, groups_y, second, *refs):
    if second:
        old, refs = refs[0], refs[1:]
    (field, part_ref, inflow, result, samp_ref,
     y_send, y_recv, x_recv, gathered, mine, send_sem, recv_sem) = refs
    comps, cells_x, cells_y, depth = field.shape
    tile_x, tile_y = lax.axis_index("gx"), lax.axis_index("gy")
    last_x = groups_x - 1

    def peer(k):
        return lax.rem(tile_y + k, groups_y)

    north, south = peer(1), peer(groups_y - 1)
    barrier = pltpu.get_barrier_semaphore()
    for k in range(1, groups_y):
        pl.semaphore_signal(barrier, inc=1, device_id={"gy": peer(k)}, device_id_type=MESH)

    @pl.when(tile_x > 0)
    def _():
        pl.semaphore_signal(barrier, inc=1, device_id={"gx": tile_x - 1}, device_id_type=MESH)

    @pl.when(tile_x < last_x)
    def _():
        pl.semaphore_signal(barrier, inc=1, device_id={"gx": tile_x + 1}, device_id_type=MESH)

    @pl.loop(0, cells_x // 8)
    def _(block):
        rows = pl.ds(block * 8, 8)
        for c in range(comps):
            for half in range(2):
                lanes = pl.ds(half * LANES, LANES)
                y_send[0, half, c, rows, :] = field[c, rows, 0, lanes]
                y_send[1, half, c, rows, :] = field[c, rows, cells_y - 1, lanes]

    @pl.when(tile_x == 0)
    def _():
        x_recv[0] = inflow[...]

    @pl.when(tile_x == last_x)
    def _():
        x_recv[1] = field[:, cells_x - 1]

    neighbours = (tile_x > 0).astype(I32) + (tile_x < last_x).astype(I32)
    pl.semaphore_wait(barrier, groups_y - 1 + neighbours)

    def remote(src, dst, slot, where):
        return pltpu.make_async_remote_copy(
            src_ref=src, dst_ref=dst, send_sem=send_sem.at[slot], recv_sem=recv_sem.at[slot],
            device_id=where, device_id_type=MESH,
        )

    def part_copy(k):
        return remote(part_ref.at[peer(k)], gathered.at[k - 1], k - 1, {"gy": peer(k)})

    def sum_copy(k, owner):
        return remote(mine, samp_ref.at[owner], groups_y + k - 2, {"gy": peer(k)})

    base = groups_y - 1
    to_north = remote(y_send.at[1], y_recv.at[0], 2 * base, {"gy": north})
    to_south = remote(y_send.at[0], y_recv.at[1], 2 * base + 1, {"gy": south})
    to_east = remote(field.at[:, cells_x - 1], x_recv.at[0], 2 * base + 2, {"gx": tile_x + 1})
    to_west = remote(field.at[:, 0], x_recv.at[1], 2 * base + 3, {"gx": tile_x - 1})

    for k in range(1, groups_y):
        part_copy(k).start()
    to_north.start()
    to_south.start()

    @pl.when(tile_x < last_x)
    def _():
        to_east.start()

    @pl.when(tile_x > 0)
    def _():
        to_west.start()

    scale = 0.5 if second else 1.0
    a = scale * TIME_STEP * VISCOSITY
    b = scale * TIME_STEP * 0.5
    centre = scale * (1.0 - 6.0 * TIME_STEP * VISCOSITY)
    sub = lax.broadcasted_iota(I32, (8, LANES), 0)
    lane = lax.broadcasted_iota(I32, (8, LANES), 1)
    first_row, last_row = sub == 0, sub == 7
    first_lane, last_lane = lane == 0, lane == LANES - 1
    zero = jnp.zeros((8, LANES), F32)
    halves = [pl.ds(half * LANES, LANES) for half in range(2)]
    strips = cells_y // 8

    def tile(c, i, t, half):
        return field[c, i, pl.ds(8 * t, 8), halves[half]]

    def ghost(side, half, c, i):
        return y_recv[side, half, c, pl.ds(i, 8, stride=0), :]

    def plane(i, west, east, ghosts):
        for t in range(strips):
            rows = pl.ds(8 * t, 8)
            here = [[tile(c, i, t, half) for half in range(2)] for c in range(comps)]
            lower, upper = [], []
            for c in range(comps):
                up = [pltpu.roll(v, 1, 1) for v in here[c]]
                down = [pltpu.roll(v, LANES - 1, 1) for v in here[c]]
                lower.append([jnp.where(first_lane, zero, up[0]), jnp.where(first_lane, up[0], up[1])])
                upper.append([jnp.where(last_lane, down[1], down[0]), jnp.where(last_lane, zero, down[1])])
            for half in range(2):
                bu, bv, bw = (b * here[c][half] for c in range(3))
                for c in range(comps):
                    if t > 0:
                        below = pltpu.roll(tile(c, i, t - 1, half), 1, 0)
                    else:
                        below = ghost(0, half, c, i) if ghosts else zero
                    if t < strips - 1:
                        above = pltpu.roll(tile(c, i, t + 1, half), 7, 0)
                    else:
                        above = ghost(1, half, c, i) if ghosts else zero
                    value = here[c][half]
                    to_s = jnp.where(first_row, below, pltpu.roll(value, 1, 0))
                    to_n = jnp.where(last_row, above, pltpu.roll(value, 7, 0))
                    out = (
                        centre * value
                        + ((a - bu) * east(c, rows, halves[half]) + (a + bu) * west(c, rows, halves[half]))
                        + ((a - bv) * to_n + (a + bv) * to_s)
                        + ((a - bw) * upper[c][half] + (a + bw) * lower[c][half])
                    )
                    if second:
                        out = out + 0.5 * old[c, i, rows, halves[half]]
                    result[c, i, rows, halves[half]] = out

    def inside(i, ghosts):
        plane(
            i,
            lambda c, rows, lanes: field[c, i - 1, rows, lanes],
            lambda c, rows, lanes: field[c, i + 1, rows, lanes],
            ghosts,
        )

    def piece(start, stop, ghosts):
        @pl.loop(0, (stop - start) // STEP)
        def _(n):
            for k in range(STEP):
                inside(start + n * STEP + k, ghosts)

    steps = (cells_x - 2) // STEP
    cuts = [1 + STEP * (steps * k // 4) for k in (0, 2, 3, 4)]

    piece(cuts[0], cuts[1], False)
    for k in range(1, groups_y):
        part_copy(k).wait_recv()
    total = functools.reduce(jnp.add, [gathered[k] for k in range(groups_y - 1)], part_ref[tile_y])
    mine[...] = total
    samp_ref[tile_y] = total
    for k in range(1, groups_y):
        sum_copy(k, tile_y).start()
    piece(cuts[1], cuts[2], False)
    to_north.wait_recv()
    to_south.wait_recv()
    piece(cuts[2], cuts[3], True)
    for i in range(cuts[3], cells_x - 1):
        inside(i, True)

    @pl.when(tile_x > 0)
    def _():
        to_east.wait_recv()

    @pl.when(tile_x < last_x)
    def _():
        to_west.wait_recv()

    plane(
        0,
        lambda c, rows, lanes: x_recv[0, c, rows, lanes],
        lambda c, rows, lanes: field[c, 1, rows, lanes],
        True,
    )
    plane(
        cells_x - 1,
        lambda c, rows, lanes: field[c, cells_x - 2, rows, lanes],
        lambda c, rows, lanes: x_recv[1, c, rows, lanes],
        True,
    )

    @pl.loop(0, (cuts[2] - cuts[0]) // STEP)
    def _(n):
        for k in range(STEP):
            i = cuts[0] + n * STEP + k
            for side, t, mask in ((0, 0, first_row), (1, strips - 1, last_row)):
                rows = pl.ds(8 * t, 8)
                for half in range(2):
                    bv = b * tile(1, i, t, half)
                    weight = jnp.where(mask, a - bv if side else a + bv, 0.0)
                    for c in range(comps):
                        before = result[c, i, rows, halves[half]]
                        result[c, i, rows, halves[half]] = before + weight * ghost(side, half, c, i)

    for k in range(1, groups_y):
        sum_copy(k, peer(groups_y - k)).wait_recv()
    for k in range(1, groups_y):
        part_copy(k).wait_send()
        sum_copy(k, tile_y).wait_send()
    to_north.wait_send()
    to_south.wait_send()

    @pl.when(tile_x < last_x)
    def _():
        to_east.wait_send()

    @pl.when(tile_x > 0)
    def _():
        to_west.wait_send()


def local(groups_x, groups_y, velocity, inflow, positions, tiles, coefs, counts):
    comps, cells_x, cells_y, depth = velocity.shape
    total_y = cells_y * groups_y
    pos, tiles, coefs = positions[0].transpose(1, 0, 2), tiles[0].T, coefs[0]
    _, recs, points = pos.shape
    velocity, pos, tiles = (
        pltpu.with_memory_space_constraint(x, pltpu.HBM) for x in (velocity, pos, tiles)
    )
    grid = pltpu.VMEM(velocity.shape, F32)
    table = pltpu.VMEM((groups_y, comps, recs * points // (groups_y * LANES), LANES), F32)

    field, _, part, plan, picks, along = pl.pallas_call(
        functools.partial(sample_first, total_y, groups_y),
        out_shape=(
            grid,
            pltpu.VMEM(pos.shape, I32),
            table,
            pltpu.SMEM((8, LANES), I32),
            pltpu.VMEM((recs, depth, points), BF16),
            pltpu.VMEM((recs, cells_y, points), F32),
        ),
        in_specs=[HBM, HBM, HBM, SMEM],
        out_specs=(VMEM, VMEM, VMEM, SMEM, VMEM, VMEM),
        scratch_shapes=[
            pltpu.VMEM(tiles.shape, I32),
            pltpu.VMEM((8, LANES), I32),
            pltpu.SemaphoreType.DMA((CHUNKS + 3,)),
        ],
        compiler_params=params(),
        name="sample_first",
    )(velocity, pos, tiles, counts)

    def swap(second, *operands):
        sems = 2 * (groups_y - 1) + 4
        return pl.pallas_call(
            functools.partial(exchange, groups_x, groups_y, second),
            out_shape=(grid, table),
            in_specs=[VMEM] * len(operands),
            out_specs=(VMEM, VMEM),
            scratch_shapes=[
                pltpu.VMEM((2, 2, comps, cells_x, LANES), F32),
                pltpu.VMEM((2, 2, comps, cells_x, LANES), F32),
                pltpu.VMEM((2, comps, cells_y, depth), F32),
                pltpu.VMEM((groups_y - 1, *table.shape[1:]), F32),
                pltpu.VMEM(table.shape[1:], F32),
                pltpu.SemaphoreType.DMA((sems,)),
                pltpu.SemaphoreType.DMA((sems,)),
            ],
            compiler_params=params(collective_id=int(second), has_side_effects=True),
            name="exchange_second" if second else "exchange_first",
        )(*operands)

    section, samp_a = swap(False, field, part, inflow)
    section, part = pl.pallas_call(
        spread_and_sample,
        out_shape=(grid, table),
        in_specs=[SMEM] + [VMEM] * 5,
        out_specs=(VMEM, VMEM),
        input_output_aliases={5: 0},
        compiler_params=params(),
        name="spread_and_sample",
    )(plan, picks, along, coefs, samp_a, section)
    final, samp_b = swap(True, field, section, part, inflow)
    _, velocity_next, blade = pl.pallas_call(
        spread_last,
        out_shape=(
            grid,
            jax.ShapeDtypeStruct(velocity.shape, F32),
            jax.ShapeDtypeStruct(pos.shape, F32),
        ),
        in_specs=[SMEM, VMEM, VMEM, VMEM, SMEM, VMEM, VMEM, VMEM],
        out_specs=(VMEM, HBM, VMEM),
        input_output_aliases={7: 0},
        scratch_shapes=[pltpu.SemaphoreType.DMA((CHUNKS,))],
        compiler_params=params(),
        name="spread_last",
    )(plan, picks, along, coefs, counts, samp_a, samp_b, final)
    return (velocity_next, blade.transpose(1, 0, 2)[None])


def solution(mesh):
    return jax.shard_map(
        functools.partial(local, mesh.shape["gx"], mesh.shape["gy"]),
        mesh=mesh,
        in_specs=(
            P(None, "gx", "gy", None),
            P(None, "gy", None),
            P("gx", None, None, None),
            P("gx", None, None),
            P("gx", None, None),
            P("gx"),
        ),
        out_specs=(P(None, "gx", "gy", None), P("gx", None, None, None)),
        check_vma=False,
    )
```

time: 85.5 us -> 72.3 us (0.85)
  the two profiles are of different devices: /device:TPU:65 before, /device:TPU:1 now
where the time goes in v3:
time: 72.3 us; the launch traced here: 72.1 us
  Pallas kernels  63.3 us (88%)
  local copies, waits for them, and re-layouts  7.42 us (10%)
  between operations  1.38 us (2%)
    pallas_call x2, Pallas kernels, swap(): pl.pallas_call(functools.partial(exchange, groups_x, groups_y, second), o...  51.4 us
    unnamed x8, local copies, waits for them, and re-layouts  7.42 us
    pallas_call x1, Pallas kernels, local(): pl.pallas_call(functools.partial(sample_first, total_y, groups_y), out_sh...  5.09 us
    pallas_call x1, Pallas kernels, local(): pl.pallas_call(spread_last, out_shape=(grid, jax.ShapeDtypeStruct(velocit...  4.91 us
    pallas_call x1, Pallas kernels, local(): pl.pallas_call(spread_and_sample, out_shape=(grid, table), in_specs=[SMEM...  1.96 us

profile of v3, /device:TPU:1, one launch (start us, length us, event | category | flops | bytes accessed | tf_op | source)
XLA Modules:
  0.0 72.1 jit_solution(15805263273503847534)
XLA Ops:
  0.6 0.0 copy-start.2
  1.3 0.0 copy-start.3
  1.3 5.1 %sample_first.1 = (f32[3,96,32,256]{3,2,1,0:T(8,128)S(1)}, s32[3,64,256]{2,1,0:T(8,128)}, f32[16,3,8,128]{3,2,1,0:T(8,128)S(1)}, s32[8,128]{1,0:T(8,128)S(4)}, b...) custom-call(f32[3,96,32,256]{3,2,1,0:T(8,128)} %vel_hbm.1, s32[3,64,256]{2,1,0:T(8,128)} %bitcast.12, ...), custom_call_target="tpu_custom_call" | custom-call | tf_op jit(solution)/shard_map/sample_first/pallas_call | solution.py:456
  6.4 0.0 copy-done.2
  6.4 23.5 %exchange_first.1 = (f32[3,96,32,256]{3,2,1,0:T(8,128)S(1)}, f32[16,3,8,128]{3,2,1,0:T(8,128)S(1)}) custom-call(f32[3,96,32,256]{3,2,1,0:T(8,128)S(1)} %get-tuple-element.18.refs_0_, f32[16,3,8,128]{3,2,1,0:T(8,128)S(1)} %get-tuple-element.19.refs_1_, f32[3,32,256]{2,1,0:T(8,128)S(1)} %copy-done.2), custom_call_target="tpu_custom_call" | custom-call | tf_op jit(solution)/shard_map/exchange_first/pallas_call | solution.py:479
  29.9 0.0 copy-done.3
  29.9 2.0 %spread_and_sample.1 = (f32[3,96,32,256]{3,2,1,0:T(8,128)S(1)}, f32[16,3,8,128]{3,2,1,0:T(8,128)S(1)}) custom-call(s32[8,128]{1,0:T(8,128)S(4)} %get-tuple-element.15.plan_ref, bf16[64,256,256]{2,1,0:T(8,128)(2,1)S(1)} %get-tuple-element.16.pick_ref, f32[64,32,256]{2,1,0:T(8,128)S(1)} %get-tuple-element.17.along_ref, ...), custom_call_target="tpu_custom_call", output_to_operand_aliasing={{0}: (5, {})} | custom-call | tf_op jit(solution)/shard_map/spread_and_sample/pallas_call | solution.py:498
  31.9 27.9 %exchange_second.1 = (f32[3,96,32,256]{3,2,1,0:T(8,128)S(1)}, f32[16,3,8,128]{3,2,1,0:T(8,128)S(1)}) custom-call(f32[3,96,32,256]{3,2,1,0:T(8,128)S(1)} %get-tuple-element.18.refs_0_, f32[3,96,32,256]{3,2,1,0:T(8,128)S(1)} %get-tuple-element.22.refs_1_, f32[16,3,8,128]{3,2,1,0:T(8,128)S(1)} %get-tuple-element.23.refs_2_, f32[3,32,256]{2,1,0:T(8,128)S(1)} %copy-done.2), custom_call_target="tpu_custom_call" | custom-call | tf_op jit(solution)/shard_map/exchange_second/pallas_call | solution.py:479
  59.8 0.0 copy-start
  59.8 3.7 %copy-done = f32[3,96,32,256]{3,2,1,0:T(8,128)} copy-done((f32[3,96,32,256]{3,2,1,0:T(8,128)}, f32[3,96,32,256]{3,2,1,0:T(8,128)S(1)}, u32[]{:S(2)}) %copy-start) | copy-done | bytes 9437208
  63.5 0.0 copy-start.1
  63.5 3.7 %copy-done.1 = f32[3,96,32,256]{3,2,1,0:T(8,128)S(1)} copy-done((f32[3,96,32,256]{3,2,1,0:T(8,128)S(1)}, f32[3,96,32,256]{3,2,1,0:T(8,128)}, u32[]{:S(2)}) %copy-start.1) | copy-done | bytes 9437208
  67.2 4.9 %spread_last.1 = (f32[3,96,32,256]{3,2,1,0:T(8,128)S(1)}, f32[3,96,32,256]{3,2,1,0:T(8,128)}, f32[3,64,256]{2,1,0:T(8,128)}) custom-call(s32[8,128]{1,0:T(8,128)S(4)} %get-tuple-element.15.plan_ref, bf16[64,256,256]{2,1,0:T(8,128)(2,1)S(1)} %get-tuple-element.16.pick_ref, ...), custom_call_target="tpu_custom_call", output_to_operand_aliasing={{0}: (7, {})} | custom-call | tf_op jit(solution)/shard_map/spread_last/pallas_call | solution.py:508
Async XLA Ops:
  0.6 5.8 %copy-start.2 = (f32[3,32,256]{2,1,0:T(8,128)S(1)}, f32[3,32,256]{2,1,0:T(8,128)}, u32[]{:S(2)}) copy-start(f32[3,32,256]{2,1,0:T(8,128)} %refs_3_.1) | copy-start | bytes 294916
  1.3 28.6 %copy-start.3 = (f32[1,64,256]{2,1,0:T(8,128)S(1)}, f32[1,64,256]{2,1,0:T(8,128)}, u32[]{:S(2)}) copy-start(f32[1,64,256]{2,1,0:T(8,128)} %param.10) | copy-start | bytes 196612
  59.8 3.7 %copy-start = (f32[3,96,32,256]{3,2,1,0:T(8,128)}, f32[3,96,32,256]{3,2,1,0:T(8,128)S(1)}, u32[]{:S(2)}) copy-start(f32[3,96,32,256]{3,2,1,0:T(8,128)S(1)} %get-tuple-element.25._) | copy-start | bytes 28311556
  63.5 3.7 %copy-start.1 = (f32[3,96,32,256]{3,2,1,0:T(8,128)S(1)}, f32[3,96,32,256]{3,2,1,0:T(8,128)}, u32[]{:S(2)}) copy-start(f32[3,96,32,256]{3,2,1,0:T(8,128)} %copy-done) | copy-start | bytes 28311556

commit v4 on v3

--- a/solution.py
+++ b/solution.py
@@ -26,7 +26,7 @@
 
 
 def params(**kw):
-    return pltpu.CompilerParams(vmem_limit_bytes=16 << 20, **kw)
+    return pltpu.CompilerParams(vmem_limit_bytes=6 << 20, **kw)
 
 
 def local_y(pos_y, tile_y, cells_y, total_y):
@@ -49,19 +49,22 @@
     return both[:rows] + both[rows:]
 
 
-def build_tables(pos_ref, pick_ref, along_ref, n, rec, tile_y, total_y):
+def build_tables(pos_ref, pick_ref, here_ref, n, rec, tile_y, cells_y, total_y):
     depth, points = pick_ref.shape[1:]
-    cells_y = along_ref.shape[1]
     cell = lax.broadcasted_iota(I32, (depth, points), 0)
     pick_ref[n] = (cell == pos_ref[2, pl.ds(rec, 1), :]).astype(F32).astype(BF16)
-    here = local_y(pos_ref[1, pl.ds(rec, 1), :], tile_y, cells_y, total_y)
-    dist = jnp.abs(lax.broadcasted_iota(I32, (cells_y, points), 0) - here)
-    along_ref[n] = jnp.where(
+    here_ref[pl.ds(n, 1), :] = local_y(pos_ref[1, pl.ds(rec, 1), :], tile_y, cells_y, total_y)
+
+
+def weight_y(here_ref, n, cells_y):
+    here = here_ref[pl.ds(n, 1), :]
+    dist = jnp.abs(lax.broadcasted_iota(I32, (cells_y, here.shape[1]), 0) - here)
+    return jnp.where(
         dist == 0, K0, jnp.where(dist == 1, K1, jnp.where(dist == 2, K2, 0.0))
     ).astype(F32)
 
 
-def sample_pair(field, plan_ref, pick_ref, along_ref, part_ref, pair, count):
+def sample_pair(field, plan_ref, pick_ref, here_ref, part_ref, pair, count):
     comps, _, cells_y, depth = field.shape
     for n in (2 * pair, jnp.minimum(2 * pair + 1, count - 1)):
         rec, hub = plan_ref[0, n], plan_ref[1, n]
@@ -72,7 +75,7 @@
         )
         smooth = smooth_z(planes.reshape(comps * cells_y, depth))
         inner = split_dot(smooth, pick_ref[n], ((1,), (0,)))
-        value = jnp.sum(inner.reshape(comps, cells_y, -1) * along_ref[n][None], axis=1)
+        value = jnp.sum(inner.reshape(comps, cells_y, -1) * weight_y(here_ref, n, cells_y)[None], axis=1)
         group, row = rec // 8, lax.rem(rec, 8)
         for half in range(2):
             for c in range(comps):
@@ -81,7 +84,7 @@
                 ]
 
 
-def spread_pair(field, plan_ref, pick_ref, along_ref, coef_ref, samp_ref, scale, pair, count):
+def spread_pair(field, plan_ref, pick_ref, here_ref, coef_ref, samp_ref, scale, pair, count):
     comps, _, cells_y, depth = field.shape
     slabs = []
     for k in range(2):
@@ -97,7 +100,7 @@
         ]
         speed = jnp.sqrt(sampled[0] * sampled[0] + sampled[1] * sampled[1] + sampled[2] * sampled[2])
         strength = coef_ref[pl.ds(rec, 1), :] * speed * factor
-        along = along_ref[n]
+        along = weight_y(here_ref, n, cells_y)
         weighted = jnp.concatenate([along * (strength * value) for value in sampled], axis=0)
         slab = smooth_z(split_dot(weighted, pick_ref[n], ((1,), (1,))))
         slabs.append((hub, slab.reshape(comps, cells_y, depth)))
@@ -137,7 +140,7 @@
 
 
 def sample_first(total_y, groups_y, vel_hbm, pos_hbm, tiles_hbm, counts_ref,
-                 field, pos_ref, part_ref, plan_ref, pick_ref, along_ref, tiles_ref, rows_ref, sems):
+                 field, pos_ref, part_ref, plan_ref, pick_ref, here_ref, tiles_ref, rows_ref, sems):
     cells_x, cells_y = field.shape[1:3]
     tile_y = lax.axis_index("gy")
     chunk = cells_x // CHUNKS
@@ -162,7 +165,7 @@
 
     @pl.loop(0, count)
     def _(n):
-        build_tables(pos_ref, pick_ref, along_ref, n, plan_ref[0, n], tile_y, total_y)
+        build_tables(pos_ref, pick_ref, here_ref, n, plan_ref[0, n], tile_y, cells_y, total_y)
 
     start = jnp.int32(0)
     for q in range(CHUNKS):
@@ -174,47 +177,29 @@
 
         @pl.loop(start, stop)
         def _(pair):
-            sample_pair(field, plan_ref, pick_ref, along_ref, part_ref, pair, count)
+            sample_pair(field, plan_ref, pick_ref, here_ref, part_ref, pair, count)
 
         start = stop
 
 
-def spread_and_sample(plan_ref, pick_ref, along_ref, coef_ref, samp_ref, _, field, part_ref):
+def spread_and_sample(plan_ref, pick_ref, here_ref, coef_ref, samp_ref, _, field, part_ref):
     count = plan_ref[2, LANES - 1]
     part_ref[...] = jnp.zeros_like(part_ref)
 
     @pl.loop(0, (count + 1) // 2)
     def _(pair):
-        spread_pair(field, plan_ref, pick_ref, along_ref, coef_ref, samp_ref, TIME_STEP, pair, count)
+        spread_pair(field, plan_ref, pick_ref, here_ref, coef_ref, samp_ref, TIME_STEP, pair, count)
 
     @pl.loop(0, (count + 1) // 2)
     def _(pair):
-        sample_pair(field, plan_ref, pick_ref, along_ref, part_ref, pair, count)
-
-
-def spread_last(plan_ref, pick_ref, along_ref, coef_ref, counts_ref, samp_a, samp_b, _,
-                field, next_hbm, blade_ref, sems):
-    comps, recs, _ = blade_ref.shape
+        sample_pair(field, plan_ref, pick_ref, here_ref, part_ref, pair, count)
+
+
+def spread_last(plan_ref, pick_ref, here_ref, coef_ref, counts_ref, samp_a, samp_b, _,
+                field, next_hbm, blade_hbm, blade, sems):
+    comps, recs, _ = blade.shape
     chunk = field.shape[1] // CHUNKS
     count = plan_ref[2, LANES - 1]
-    start = jnp.int32(0)
-    stores = []
-    for q in range(CHUNKS):
-        if q < CHUNKS - 1:
-            stop = (plan_ref[2, (q + 1) * chunk + RAD] + 1) // 2
-        else:
-            stop = (count + 1) // 2
-
-        @pl.loop(start, stop)
-        def _(pair):
-            spread_pair(field, plan_ref, pick_ref, along_ref, coef_ref, samp_b,
-                        0.5 * TIME_STEP, pair, count)
-
-        planes = pl.ds(q * chunk, chunk)
-        stores.append(pltpu.make_async_copy(field.at[:, planes], next_hbm.at[:, planes], sems.at[q]))
-        stores[-1].start()
-        start = stop
-
     for half in range(2):
         lanes = pl.ds(half * LANES, LANES)
         for group in range(recs // 8):
@@ -226,9 +211,30 @@
             rec = group * 8 + lax.broadcasted_iota(I32, (8, LANES), 0)
             strength = jnp.where(rec < counts_ref[0], coef_ref[rows, lanes] * -0.5, 0.0)
             for c in range(comps):
-                blade_ref[c, rows, lanes] = strength * (speed_a * a[c] + speed_b * b[c])
+                blade[c, rows, lanes] = strength * (speed_a * a[c] + speed_b * b[c])
+    put = pltpu.make_async_copy(blade, blade_hbm, sems.at[CHUNKS])
+    put.start()
+    start = jnp.int32(0)
+    stores = []
+    for q in range(CHUNKS):
+        if q < CHUNKS - 1:
+            stop = (plan_ref[2, (q + 1) * chunk + RAD] + 1) // 2
+        else:
+            stop = (count + 1) // 2
+
+        @pl.loop(start, stop)
+        def _(pair):
+            spread_pair(field, plan_ref, pick_ref, here_ref, coef_ref, samp_b,
+                        0.5 * TIME_STEP, pair, count)
+
+        planes = pl.ds(q * chunk, chunk)
+        stores.append(pltpu.make_async_copy(field.at[:, planes], next_hbm.at[:, planes], sems.at[q]))
+        stores[-1].start()
+        start = stop
+
     for store in stores:
         store.wait()
+    put.wait()
 
 
 def exchange(groups_x, groups_y, second, *refs):
@@ -453,7 +459,7 @@
     grid = pltpu.VMEM(velocity.shape, F32)
     table = pltpu.VMEM((groups_y, comps, recs * points // (groups_y * LANES), LANES), F32)
 
-    field, _, part, plan, picks, along = pl.pallas_call(
+    field, _, part, plan, picks, here = pl.pallas_call(
         functools.partial(sample_first, total_y, groups_y),
         out_shape=(
             grid,
@@ -461,7 +467,7 @@
             table,
             pltpu.SMEM((8, LANES), I32),
             pltpu.VMEM((recs, depth, points), BF16),
-            pltpu.VMEM((recs, cells_y, points), F32),
+            pltpu.VMEM((recs, points), I32),
         ),
         in_specs=[HBM, HBM, HBM, SMEM],
         out_specs=(VMEM, VMEM, VMEM, SMEM, VMEM, VMEM),
@@ -503,7 +509,7 @@
         input_output_aliases={5: 0},
         compiler_params=params(),
         name="spread_and_sample",
-    )(plan, picks, along, coefs, samp_a, section)
+    )(plan, picks, here, coefs, samp_a, section)
     final, samp_b = swap(True, field, section, part, inflow)
     _, velocity_next, blade = pl.pallas_call(
         spread_last,
@@ -513,12 +519,12 @@
             jax.ShapeDtypeStruct(pos.shape, F32),
         ),
         in_specs=[SMEM, VMEM, VMEM, VMEM, SMEM, VMEM, VMEM, VMEM],
-        out_specs=(VMEM, HBM, VMEM),
+        out_specs=(VMEM, HBM, HBM),
         input_output_aliases={7: 0},
-        scratch_shapes=[pltpu.SemaphoreType.DMA((CHUNKS,))],
+        scratch_shapes=[pltpu.VMEM(pos.shape, F32), pltpu.SemaphoreType.DMA((CHUNKS + 1,))],
         compiler_params=params(),
         name="spread_last",
-    )(plan, picks, along, coefs, counts, samp_a, samp_b, final)
+    )(plan, picks, here, coefs, counts, samp_a, samp_b, final)
     return (velocity_next, blade.transpose(1, 0, 2)[None])
 
 

time: 72.3 us -> 62.3 us (0.86)
  local copies, waits for them, and re-layouts: 7.42 us -> 0.01 us
  Pallas kernels: 63.3 us -> 60.8 us
    unnamed x8 -> x4, local copies, waits for them, and re-layouts: 7.42 us -> 0.01 us
    pallas_call x1, Pallas kernels: 4.91 us -> 3.87 us  [local(): pl.pallas_call(spread_last, out_shape=(grid, jax.ShapeDtypeStruct(velocit...]
    pallas_call x1, Pallas kernels: 1.96 us -> 0.99 us  [local(): pl.pallas_call(spread_and_sample, out_shape=(grid, table), in_specs=[SMEM...]
where the time goes in v4:
time: 62.3 us; the launch traced here: 62.2 us
  Pallas kernels  60.8 us (98%)
  between operations  1.37 us (2%)
    pallas_call x2, Pallas kernels, swap(): pl.pallas_call(functools.partial(exchange, groups_x, groups_y, second), o...  50.8 us
    pallas_call x1, Pallas kernels, local(): pl.pallas_call(functools.partial(sample_first, total_y, groups_y), out_sh...  5.1 us
    pallas_call x1, Pallas kernels, local(): pl.pallas_call(spread_last, out_shape=(grid, jax.ShapeDtypeStruct(velocit...  3.87 us

profile of v4, /device:TPU:1, one launch (start us, length us, event | category | flops | bytes accessed | tf_op | source)
XLA Modules:
  0.0 62.2 jit_solution(15122518678399388571)
XLA Ops:
  0.6 0.0 copy-start
  1.3 0.0 copy-start.1
  1.3 5.1 %sample_first.1 = (f32[3,96,32,256]{3,2,1,0:T(8,128)S(1)}, s32[3,64,256]{2,1,0:T(8,128)}, f32[16,3,8,128]{3,2,1,0:T(8,128)S(1)}, s32[8,128]{1,0:T(8,128)S(4)}, b...) custom-call(f32[3,96,32,256]{3,2,1,0:T(8,128)} %vel_hbm.1, s32[3,64,256]{2,1,0:T(8,128)} %bitcast.12, ...), custom_call_target="tpu_custom_call" | custom-call | tf_op jit(solution)/shard_map/sample_first/pallas_call | solution.py:462
  6.4 0.0 copy-done
  6.4 22.3 %exchange_first.1 = (f32[3,96,32,256]{3,2,1,0:T(8,128)S(1)}, f32[16,3,8,128]{3,2,1,0:T(8,128)S(1)}) custom-call(f32[3,96,32,256]{3,2,1,0:T(8,128)S(1)} %get-tuple-element.18.refs_0_, f32[16,3,8,128]{3,2,1,0:T(8,128)S(1)} %get-tuple-element.19.refs_1_, f32[3,32,256]{2,1,0:T(8,128)S(1)} %copy-done), custom_call_target="tpu_custom_call" | custom-call | tf_op jit(solution)/shard_map/exchange_first/pallas_call | solution.py:485
  28.8 0.0 copy-done.1
  28.8 1.0 %spread_and_sample.1 = (f32[3,96,32,256]{3,2,1,0:T(8,128)S(1)}, f32[16,3,8,128]{3,2,1,0:T(8,128)S(1)}) custom-call(s32[8,128]{1,0:T(8,128)S(4)} %get-tuple-element.15.plan_ref, bf16[64,256,256]{2,1,0:T(8,128)(2,1)S(1)} %get-tuple-element.16.pick_ref, s32[64,256]{1,0:T(8,128)S(1)} %get-tuple-element.17.here_ref, ...), custom_call_target="tpu_custom_call", output_to_operand_aliasing={{0}: (5, {})} | custom-call | tf_op jit(solution)/shard_map/spread_and_sample/pallas_call | solution.py:504
  29.8 28.5 %exchange_second.1 = (f32[3,96,32,256]{3,2,1,0:T(8,128)S(1)}, f32[16,3,8,128]{3,2,1,0:T(8,128)S(1)}) custom-call(f32[3,96,32,256]{3,2,1,0:T(8,128)S(1)} %get-tuple-element.18.refs_0_, f32[3,96,32,256]{3,2,1,0:T(8,128)S(1)} %get-tuple-element.22.refs_1_, f32[16,3,8,128]{3,2,1,0:T(8,128)S(1)} %get-tuple-element.23.refs_2_, f32[3,32,256]{2,1,0:T(8,128)S(1)} %copy-done), custom_call_target="tpu_custom_call" | custom-call | tf_op jit(solution)/shard_map/exchange_second/pallas_call | solution.py:485
  58.3 3.9 %spread_last.1 = (f32[3,96,32,256]{3,2,1,0:T(8,128)S(1)}, f32[3,96,32,256]{3,2,1,0:T(8,128)}, f32[3,64,256]{2,1,0:T(8,128)}) custom-call(s32[8,128]{1,0:T(8,128)S(4)} %get-tuple-element.15.plan_ref, bf16[64,256,256]{2,1,0:T(8,128)(2,1)S(1)} %get-tuple-element.16.pick_ref, s32[64,256]{1,0:T(8,128)S(1)} %get-tuple-element.17.here_ref, ...), custom_call_target="tpu_custom_call", output_to_operand_aliasing={{0}: (7, {})} | custom-call | tf_op jit(solution)/shard_map/spread_last/pallas_call | solution.py:514
Async XLA Ops:
  0.6 5.8 %copy-start = (f32[3,32,256]{2,1,0:T(8,128)S(1)}, f32[3,32,256]{2,1,0:T(8,128)}, u32[]{:S(2)}) copy-start(f32[3,32,256]{2,1,0:T(8,128)} %refs_3_.1) | copy-start | bytes 294916
  1.3 27.5 %copy-start.1 = (f32[1,64,256]{2,1,0:T(8,128)S(1)}, f32[1,64,256]{2,1,0:T(8,128)}, u32[]{:S(2)}) copy-start(f32[1,64,256]{2,1,0:T(8,128)} %param.10) | copy-start | bytes 196612

commit v5 on v4

--- a/solution.py
+++ b/solution.py
@@ -21,6 +21,7 @@
 SMEM = pl.BlockSpec(memory_space=pltpu.SMEM)
 HBM = pl.BlockSpec(memory_space=pltpu.HBM)
 LANES = 128
+GROUP = 4
 STEP = 4
 CHUNKS = 4
 
@@ -64,9 +65,10 @@
     ).astype(F32)
 
 
-def sample_pair(field, plan_ref, pick_ref, here_ref, part_ref, pair, count):
+def sample_group(size, field, plan_ref, pick_ref, here_ref, part_ref, group_at, count):
     comps, _, cells_y, depth = field.shape
-    for n in (2 * pair, jnp.minimum(2 * pair + 1, count - 1)):
+    for k in range(size):
+        n = jnp.minimum(size * group_at + k, count - 1)
         rec, hub = plan_ref[0, n], plan_ref[1, n]
         planes = (
             K0 * field[:, hub]
@@ -84,13 +86,13 @@
                 ]
 
 
-def spread_pair(field, plan_ref, pick_ref, here_ref, coef_ref, samp_ref, scale, pair, count):
+def spread_group(size, field, plan_ref, pick_ref, here_ref, coef_ref, samp_ref, scale, group_at, count):
     comps, _, cells_y, depth = field.shape
     slabs = []
-    for k in range(2):
-        n = jnp.minimum(2 * pair + k, count - 1)
+    for k in range(size):
+        n = jnp.minimum(size * group_at + k, count - 1)
         rec, hub = plan_ref[0, n], plan_ref[1, n]
-        factor = jnp.where(2 * pair + k < count, -scale, 0.0)
+        factor = jnp.where(size * group_at + k < count, -scale, 0.0)
         group, row = rec // 8, lax.rem(rec, 8)
         sampled = [
             jnp.concatenate(
@@ -167,32 +169,42 @@
     def _(n):
         build_tables(pos_ref, pick_ref, here_ref, n, plan_ref[0, n], tile_y, cells_y, total_y)
 
+    def sample(size):
+        def body(at):
+            sample_group(size, field, plan_ref, pick_ref, here_ref, part_ref, at, count)
+
+        return body
+
     start = jnp.int32(0)
     for q in range(CHUNKS):
         loads[q].wait()
-        if q < CHUNKS - 1:
-            stop = plan_ref[2, (q + 1) * chunk - RAD] // 2
-        else:
-            stop = (count + 1) // 2
-
-        @pl.loop(start, stop)
-        def _(pair):
-            sample_pair(field, plan_ref, pick_ref, here_ref, part_ref, pair, count)
-
+        stop = (count if q == CHUNKS - 1 else plan_ref[2, (q + 1) * chunk - RAD]) // GROUP
+        pl.loop(start, stop)(sample(GROUP))
         start = stop
+    pl.loop(start * (GROUP // 2), (count + 1) // 2)(sample(2))
 
 
 def spread_and_sample(plan_ref, pick_ref, here_ref, coef_ref, samp_ref, _, field, part_ref):
     count = plan_ref[2, LANES - 1]
     part_ref[...] = jnp.zeros_like(part_ref)
 
-    @pl.loop(0, (count + 1) // 2)
-    def _(pair):
-        spread_pair(field, plan_ref, pick_ref, here_ref, coef_ref, samp_ref, TIME_STEP, pair, count)
-
-    @pl.loop(0, (count + 1) // 2)
-    def _(pair):
-        sample_pair(field, plan_ref, pick_ref, here_ref, part_ref, pair, count)
+    def spread(size):
+        def body(at):
+            spread_group(size, field, plan_ref, pick_ref, here_ref, coef_ref, samp_ref, TIME_STEP,
+                         at, count)
+
+        return body
+
+    def sample(size):
+        def body(at):
+            sample_group(size, field, plan_ref, pick_ref, here_ref, part_ref, at, count)
+
+        return body
+
+    full = count // GROUP
+    for step in (spread, sample):
+        pl.loop(0, full)(step(GROUP))
+        pl.loop(full * (GROUP // 2), (count + 1) // 2)(step(2))
 
 
 def spread_last(plan_ref, pick_ref, here_ref, coef_ref, counts_ref, samp_a, samp_b, _,
@@ -217,15 +229,13 @@
     start = jnp.int32(0)
     stores = []
     for q in range(CHUNKS):
-        if q < CHUNKS - 1:
-            stop = (plan_ref[2, (q + 1) * chunk + RAD] + 1) // 2
-        else:
-            stop = (count + 1) // 2
+        upto = count if q == CHUNKS - 1 else plan_ref[2, (q + 1) * chunk + RAD]
+        stop = (upto + GROUP - 1) // GROUP
 
         @pl.loop(start, stop)
-        def _(pair):
-            spread_pair(field, plan_ref, pick_ref, here_ref, coef_ref, samp_b,
-                        0.5 * TIME_STEP, pair, count)
+        def _(at):
+            spread_group(GROUP, field, plan_ref, pick_ref, here_ref, coef_ref, samp_b,
+                         0.5 * TIME_STEP, at, count)
 
         planes = pl.ds(q * chunk, chunk)
         stores.append(pltpu.make_async_copy(field.at[:, planes], next_hbm.at[:, planes], sems.at[q]))
@@ -295,15 +305,21 @@
         return remote(mine, samp_ref.at[owner], groups_y + k - 2, {"gy": peer(k)})
 
     base = groups_y - 1
-    to_north = remote(y_send.at[1], y_recv.at[0], 2 * base, {"gy": north})
-    to_south = remote(y_send.at[0], y_recv.at[1], 2 * base + 1, {"gy": south})
-    to_east = remote(field.at[:, cells_x - 1], x_recv.at[0], 2 * base + 2, {"gx": tile_x + 1})
-    to_west = remote(field.at[:, 0], x_recv.at[1], 2 * base + 3, {"gx": tile_x - 1})
+    chunk = cells_x // CHUNKS
+
+    def y_copy(q, side):
+        rows = pl.ds(q * chunk, chunk)
+        return remote(y_send.at[1 - side, :, :, rows, :], y_recv.at[side, :, :, rows, :],
+                      2 * base + 2 + 2 * q + side, {"gy": south if side else north})
+
+    to_east = remote(field.at[:, cells_x - 1], x_recv.at[0], 2 * base, {"gx": tile_x + 1})
+    to_west = remote(field.at[:, 0], x_recv.at[1], 2 * base + 1, {"gx": tile_x - 1})
 
     for k in range(1, groups_y):
         part_copy(k).start()
-    to_north.start()
-    to_south.start()
+    for q in range(CHUNKS):
+        for side in range(2):
+            y_copy(q, side).start()
 
     @pl.when(tile_x < last_x)
     def _():
@@ -331,7 +347,7 @@
     def ghost(side, half, c, i):
         return y_recv[side, half, c, pl.ds(i, 8, stride=0), :]
 
-    def plane(i, west, east, ghosts):
+    def plane(i, west, east):
         for t in range(strips):
             rows = pl.ds(8 * t, 8)
             here = [[tile(c, i, t, half) for half in range(2)] for c in range(comps)]
@@ -347,11 +363,11 @@
                     if t > 0:
                         below = pltpu.roll(tile(c, i, t - 1, half), 1, 0)
                     else:
-                        below = ghost(0, half, c, i) if ghosts else zero
+                        below = zero
                     if t < strips - 1:
                         above = pltpu.roll(tile(c, i, t + 1, half), 7, 0)
                     else:
-                        above = ghost(1, half, c, i) if ghosts else zero
+                        above = zero
                     value = here[c][half]
                     to_s = jnp.where(first_row, below, pltpu.roll(value, 1, 0))
                     to_n = jnp.where(last_row, above, pltpu.roll(value, 7, 0))
@@ -365,24 +381,23 @@
                         out = out + 0.5 * old[c, i, rows, halves[half]]
                     result[c, i, rows, halves[half]] = out
 
-    def inside(i, ghosts):
+    def inside(i):
         plane(
             i,
             lambda c, rows, lanes: field[c, i - 1, rows, lanes],
             lambda c, rows, lanes: field[c, i + 1, rows, lanes],
-            ghosts,
         )
 
-    def piece(start, stop, ghosts):
+    def piece(start, stop):
         @pl.loop(0, (stop - start) // STEP)
         def _(n):
             for k in range(STEP):
-                inside(start + n * STEP + k, ghosts)
+                inside(start + n * STEP + k)
 
     steps = (cells_x - 2) // STEP
-    cuts = [1 + STEP * (steps * k // 4) for k in (0, 2, 3, 4)]
-
-    piece(cuts[0], cuts[1], False)
+    cuts = [1 + STEP * (steps * k // 4) for k in (0, 2, 4)]
+
+    piece(cuts[0], cuts[1])
     for k in range(1, groups_y):
         part_copy(k).wait_recv()
     total = functools.reduce(jnp.add, [gathered[k] for k in range(groups_y - 1)], part_ref[tile_y])
@@ -390,12 +405,9 @@
     samp_ref[tile_y] = total
     for k in range(1, groups_y):
         sum_copy(k, tile_y).start()
-    piece(cuts[1], cuts[2], False)
-    to_north.wait_recv()
-    to_south.wait_recv()
-    piece(cuts[2], cuts[3], True)
-    for i in range(cuts[3], cells_x - 1):
-        inside(i, True)
+    piece(cuts[1], cuts[2])
+    for i in range(cuts[2], cells_x - 1):
+        inside(i)
 
     @pl.when(tile_x > 0)
     def _():
@@ -409,35 +421,38 @@
         0,
         lambda c, rows, lanes: x_recv[0, c, rows, lanes],
         lambda c, rows, lanes: field[c, 1, rows, lanes],
-        True,
     )
     plane(
         cells_x - 1,
         lambda c, rows, lanes: field[c, cells_x - 2, rows, lanes],
         lambda c, rows, lanes: x_recv[1, c, rows, lanes],
-        True,
     )
 
-    @pl.loop(0, (cuts[2] - cuts[0]) // STEP)
-    def _(n):
-        for k in range(STEP):
-            i = cuts[0] + n * STEP + k
-            for side, t, mask in ((0, 0, first_row), (1, strips - 1, last_row)):
-                rows = pl.ds(8 * t, 8)
-                for half in range(2):
-                    bv = b * tile(1, i, t, half)
-                    weight = jnp.where(mask, a - bv if side else a + bv, 0.0)
-                    for c in range(comps):
-                        before = result[c, i, rows, halves[half]]
-                        result[c, i, rows, halves[half]] = before + weight * ghost(side, half, c, i)
+    for q in range(CHUNKS):
+        for side in range(2):
+            y_copy(q, side).wait_recv()
+
+        @pl.loop(0, chunk // STEP)
+        def _(n):
+            for k in range(STEP):
+                i = q * chunk + n * STEP + k
+                for side, t, mask in ((0, 0, first_row), (1, strips - 1, last_row)):
+                    rows = pl.ds(8 * t, 8)
+                    for half in range(2):
+                        bv = b * tile(1, i, t, half)
+                        weight = jnp.where(mask, a - bv if side else a + bv, 0.0)
+                        for c in range(comps):
+                            before = result[c, i, rows, halves[half]]
+                            result[c, i, rows, halves[half]] = before + weight * ghost(side, half, c, i)
 
     for k in range(1, groups_y):
         sum_copy(k, peer(groups_y - k)).wait_recv()
     for k in range(1, groups_y):
         part_copy(k).wait_send()
         sum_copy(k, tile_y).wait_send()
-    to_north.wait_send()
-    to_south.wait_send()
+    for q in range(CHUNKS):
+        for side in range(2):
+            y_copy(q, side).wait_send()
 
     @pl.when(tile_x < last_x)
     def _():
@@ -481,7 +496,7 @@
     )(velocity, pos, tiles, counts)
 
     def swap(second, *operands):
-        sems = 2 * (groups_y - 1) + 4
+        sems = 2 * (groups_y - 1) + 2 + 2 * CHUNKS
         return pl.pallas_call(
             functools.partial(exchange, groups_x, groups_y, second),
             out_shape=(grid, table),

time: 62.3 us -> 58.5 us (0.939)
  the two profiles are of different devices: /device:TPU:1 before, /device:TPU:16 now
where the time goes in v5:
time: 58.5 us; the launch traced here: 58.4 us
  Pallas kernels  57 us (97%)
  between operations  1.37 us (2%)
    pallas_call x2, Pallas kernels, swap(): pl.pallas_call(functools.partial(exchange, groups_x, groups_y, second), o...  44.2 us
    pallas_call x1, Pallas kernels, local(): pl.pallas_call(functools.partial(sample_first, total_y, groups_y), out_sh...  5.76 us
    pallas_call x1, Pallas kernels, local(): pl.pallas_call(spread_last, out_shape=(grid, jax.ShapeDtypeStruct(velocit...  4.57 us
    pallas_call x1, Pallas kernels, local(): pl.pallas_call(spread_and_sample, out_shape=(grid, table), in_specs=[SMEM...  2.43 us

profile of v5, /device:TPU:16, one launch (start us, length us, event | category | flops | bytes accessed | tf_op | source)
XLA Modules:
  0.0 58.4 jit_solution(15643785096740176517)
XLA Ops:
  0.6 0.0 copy-start
  1.3 0.0 copy-start.1
  1.3 5.8 %sample_first.1 = (f32[3,96,32,256]{3,2,1,0:T(8,128)S(1)}, s32[3,64,256]{2,1,0:T(8,128)}, f32[16,3,8,128]{3,2,1,0:T(8,128)S(1)}, s32[8,128]{1,0:T(8,128)S(4)}, b...) custom-call(f32[3,96,32,256]{3,2,1,0:T(8,128)} %vel_hbm.1, s32[3,64,256]{2,1,0:T(8,128)} %bitcast.12, ...), custom_call_target="tpu_custom_call" | custom-call | tf_op jit(solution)/shard_map/sample_first/pallas_call | solution.py:477
  7.1 0.0 copy-done
  7.1 22.7 %exchange_first.1 = (f32[3,96,32,256]{3,2,1,0:T(8,128)S(1)}, f32[16,3,8,128]{3,2,1,0:T(8,128)S(1)}) custom-call(f32[3,96,32,256]{3,2,1,0:T(8,128)S(1)} %get-tuple-element.18.refs_0_, f32[16,3,8,128]{3,2,1,0:T(8,128)S(1)} %get-tuple-element.19.refs_1_, f32[3,32,256]{2,1,0:T(8,128)S(1)} %copy-done), custom_call_target="tpu_custom_call" | custom-call | tf_op jit(solution)/shard_map/exchange_first/pallas_call | solution.py:500
  29.8 0.0 copy-done.1
  29.9 2.4 %spread_and_sample.1 = (f32[3,96,32,256]{3,2,1,0:T(8,128)S(1)}, f32[16,3,8,128]{3,2,1,0:T(8,128)S(1)}) custom-call(s32[8,128]{1,0:T(8,128)S(4)} %get-tuple-element.15.plan_ref, bf16[64,256,256]{2,1,0:T(8,128)(2,1)S(1)} %get-tuple-element.16.pick_ref, s32[64,256]{1,0:T(8,128)S(1)} %get-tuple-element.17.here_ref, ...), custom_call_target="tpu_custom_call", output_to_operand_aliasing={{0}: (5, {})} | custom-call | tf_op jit(solution)/shard_map/spread_and_sample/pallas_call | solution.py:519
  32.3 21.5 %exchange_second.1 = (f32[3,96,32,256]{3,2,1,0:T(8,128)S(1)}, f32[16,3,8,128]{3,2,1,0:T(8,128)S(1)}) custom-call(f32[3,96,32,256]{3,2,1,0:T(8,128)S(1)} %get-tuple-element.18.refs_0_, f32[3,96,32,256]{3,2,1,0:T(8,128)S(1)} %get-tuple-element.22.refs_1_, f32[16,3,8,128]{3,2,1,0:T(8,128)S(1)} %get-tuple-element.23.refs_2_, f32[3,32,256]{2,1,0:T(8,128)S(1)} %copy-done), custom_call_target="tpu_custom_call" | custom-call | tf_op jit(solution)/shard_map/exchange_second/pallas_call | solution.py:500
  53.8 4.6 %spread_last.1 = (f32[3,96,32,256]{3,2,1,0:T(8,128)S(1)}, f32[3,96,32,256]{3,2,1,0:T(8,128)}, f32[3,64,256]{2,1,0:T(8,128)}) custom-call(s32[8,128]{1,0:T(8,128)S(4)} %get-tuple-element.15.plan_ref, bf16[64,256,256]{2,1,0:T(8,128)(2,1)S(1)} %get-tuple-element.16.pick_ref, s32[64,256]{1,0:T(8,128)S(1)} %get-tuple-element.17.here_ref, ...), custom_call_target="tpu_custom_call", output_to_operand_aliasing={{0}: (7, {})} | custom-call | tf_op jit(solution)/shard_map/spread_last/pallas_call | solution.py:529
Async XLA Ops:
  0.6 6.5 %copy-start = (f32[3,32,256]{2,1,0:T(8,128)S(1)}, f32[3,32,256]{2,1,0:T(8,128)}, u32[]{:S(2)}) copy-start(f32[3,32,256]{2,1,0:T(8,128)} %refs_3_.1) | copy-start | bytes 294916
  1.3 28.5 %copy-start.1 = (f32[1,64,256]{2,1,0:T(8,128)S(1)}, f32[1,64,256]{2,1,0:T(8,128)}, u32[]{:S(2)}) copy-start(f32[1,64,256]{2,1,0:T(8,128)} %param.10) | copy-start | bytes 196612

commit v6 on v5

--- a/solution.py
+++ b/solution.py
@@ -66,16 +66,18 @@
 
 
 def sample_group(size, field, plan_ref, pick_ref, here_ref, part_ref, group_at, count):
-    comps, _, cells_y, depth = field.shape
+    _, comps, _, cells_y, _ = field.shape
     for k in range(size):
         n = jnp.minimum(size * group_at + k, count - 1)
         rec, hub = plan_ref[0, n], plan_ref[1, n]
-        planes = (
-            K0 * field[:, hub]
-            + K1 * (field[:, hub - 1] + field[:, hub + 1])
-            + K2 * (field[:, hub - 2] + field[:, hub + 2])
-        )
-        smooth = smooth_z(planes.reshape(comps * cells_y, depth))
+        planes = [
+            K0 * field[half, :, hub]
+            + K1 * (field[half, :, hub - 1] + field[half, :, hub + 1])
+            + K2 * (field[half, :, hub - 2] + field[half, :, hub + 2])
+            for half in range(2)
+        ]
+        planes = [value.reshape(comps * cells_y, LANES) for value in planes]
+        smooth = smooth_z(jnp.concatenate(planes, axis=1))
         inner = split_dot(smooth, pick_ref[n], ((1,), (0,)))
         value = jnp.sum(inner.reshape(comps, cells_y, -1) * weight_y(here_ref, n, cells_y)[None], axis=1)
         group, row = rec // 8, lax.rem(rec, 8)
@@ -87,7 +89,7 @@
 
 
 def spread_group(size, field, plan_ref, pick_ref, here_ref, coef_ref, samp_ref, scale, group_at, count):
-    comps, _, cells_y, depth = field.shape
+    _, comps, _, cells_y, _ = field.shape
     slabs = []
     for k in range(size):
         n = jnp.minimum(size * group_at + k, count - 1)
@@ -105,10 +107,12 @@
         along = weight_y(here_ref, n, cells_y)
         weighted = jnp.concatenate([along * (strength * value) for value in sampled], axis=0)
         slab = smooth_z(split_dot(weighted, pick_ref[n], ((1,), (1,))))
-        slabs.append((hub, slab.reshape(comps, cells_y, depth)))
-    for hub, slab in slabs:
+        for half in range(2):
+            part = slab[:, half * LANES : (half + 1) * LANES]
+            slabs.append((half, hub, part.reshape(comps, cells_y, LANES)))
+    for half, hub, slab in slabs:
         for d, weight in ((-2, K2), (-1, K1), (0, K0), (1, K1), (2, K2)):
-            field[:, hub + d] += weight * slab
+            field[half, :, hub + d] += weight * slab
 
 
 def make_plan(total_y, groups_y, pos_ref, tiles_ref, counts_ref, rows_ref, cells_x, cells_y):
@@ -143,24 +147,28 @@
 
 def sample_first(total_y, groups_y, vel_hbm, pos_hbm, tiles_hbm, counts_ref,
                  field, pos_ref, part_ref, plan_ref, pick_ref, here_ref, tiles_ref, rows_ref, sems):
-    cells_x, cells_y = field.shape[1:3]
+    cells_x, cells_y = field.shape[2:4]
     tile_y = lax.axis_index("gy")
     chunk = cells_x // CHUNKS
-    fetch_pos = pltpu.make_async_copy(pos_hbm, pos_ref, sems.at[CHUNKS])
-    fetch_tiles = pltpu.make_async_copy(tiles_hbm, tiles_ref, sems.at[CHUNKS + 1])
+    fetch_pos = pltpu.make_async_copy(pos_hbm, pos_ref, sems.at[2 * CHUNKS])
+    fetch_tiles = pltpu.make_async_copy(tiles_hbm, tiles_ref, sems.at[2 * CHUNKS + 1])
     fetch_pos.start()
     fetch_tiles.start()
     loads = []
     for q in range(CHUNKS):
         planes = pl.ds(q * chunk, chunk)
-        loads.append(pltpu.make_async_copy(vel_hbm.at[:, planes], field.at[:, planes], sems.at[q]))
-        loads[-1].start()
+        for half in range(2):
+            lanes = pl.ds(half * LANES, LANES)
+            loads.append(pltpu.make_async_copy(
+                vel_hbm.at[:, planes, :, lanes], field.at[half, :, planes], sems.at[2 * q + half]
+            ))
+            loads[-1].start()
     part_ref[...] = jnp.zeros_like(part_ref)
     rows_ref[...] = jnp.zeros_like(rows_ref)
     fetch_pos.wait()
     fetch_tiles.wait()
     make_plan(total_y, groups_y, pos_ref, tiles_ref, counts_ref, rows_ref, cells_x, cells_y)
-    fetch_plan = pltpu.make_async_copy(rows_ref, plan_ref, sems.at[CHUNKS + 2])
+    fetch_plan = pltpu.make_async_copy(rows_ref, plan_ref, sems.at[2 * CHUNKS + 2])
     fetch_plan.start()
     fetch_plan.wait()
     count = plan_ref[2, LANES - 1]
@@ -177,7 +185,8 @@
 
     start = jnp.int32(0)
     for q in range(CHUNKS):
-        loads[q].wait()
+        loads[2 * q].wait()
+        loads[2 * q + 1].wait()
         stop = (count if q == CHUNKS - 1 else plan_ref[2, (q + 1) * chunk - RAD]) // GROUP
         pl.loop(start, stop)(sample(GROUP))
         start = stop
@@ -210,7 +219,7 @@
 def spread_last(plan_ref, pick_ref, here_ref, coef_ref, counts_ref, samp_a, samp_b, _,
                 field, next_hbm, blade_hbm, blade, sems):
     comps, recs, _ = blade.shape
-    chunk = field.shape[1] // CHUNKS
+    chunk = field.shape[2] // CHUNKS
     count = plan_ref[2, LANES - 1]
     for half in range(2):
         lanes = pl.ds(half * LANES, LANES)
@@ -224,7 +233,7 @@
             strength = jnp.where(rec < counts_ref[0], coef_ref[rows, lanes] * -0.5, 0.0)
             for c in range(comps):
                 blade[c, rows, lanes] = strength * (speed_a * a[c] + speed_b * b[c])
-    put = pltpu.make_async_copy(blade, blade_hbm, sems.at[CHUNKS])
+    put = pltpu.make_async_copy(blade, blade_hbm, sems.at[2 * CHUNKS])
     put.start()
     start = jnp.int32(0)
     stores = []
@@ -238,8 +247,12 @@
                          0.5 * TIME_STEP, at, count)
 
         planes = pl.ds(q * chunk, chunk)
-        stores.append(pltpu.make_async_copy(field.at[:, planes], next_hbm.at[:, planes], sems.at[q]))
-        stores[-1].start()
+        for half in range(2):
+            lanes = pl.ds(half * LANES, LANES)
+            stores.append(pltpu.make_async_copy(
+                field.at[half, :, planes], next_hbm.at[:, planes, :, lanes], sems.at[2 * q + half]
+            ))
+            stores[-1].start()
         start = stop
 
     for store in stores:
@@ -252,7 +265,7 @@
         old, refs = refs[0], refs[1:]
     (field, part_ref, inflow, result, samp_ref,
      y_send, y_recv, x_recv, gathered, mine, send_sem, recv_sem) = refs
-    comps, cells_x, cells_y, depth = field.shape
+    _, comps, cells_x, cells_y, _ = field.shape
     tile_x, tile_y = lax.axis_index("gx"), lax.axis_index("gy")
     last_x = groups_x - 1
 
@@ -277,17 +290,17 @@
         rows = pl.ds(block * 8, 8)
         for c in range(comps):
             for half in range(2):
-                lanes = pl.ds(half * LANES, LANES)
-                y_send[0, half, c, rows, :] = field[c, rows, 0, lanes]
-                y_send[1, half, c, rows, :] = field[c, rows, cells_y - 1, lanes]
+                y_send[0, half, c, rows, :] = field[half, c, rows, 0, :]
+                y_send[1, half, c, rows, :] = field[half, c, rows, cells_y - 1, :]
 
     @pl.when(tile_x == 0)
     def _():
-        x_recv[0] = inflow[...]
+        for half in range(2):
+            x_recv[0, half] = inflow[:, :, pl.ds(half * LANES, LANES)]
 
     @pl.when(tile_x == last_x)
     def _():
-        x_recv[1] = field[:, cells_x - 1]
+        x_recv[1] = field[:, :, cells_x - 1]
 
     neighbours = (tile_x > 0).astype(I32) + (tile_x < last_x).astype(I32)
     pl.semaphore_wait(barrier, groups_y - 1 + neighbours)
@@ -299,12 +312,15 @@
         )
 
     def part_copy(k):
-        return remote(part_ref.at[peer(k)], gathered.at[k - 1], k - 1, {"gy": peer(k)})
+        return remote(part_ref.at[peer(k)], gathered.at[k - 1], 0, {"gy": peer(k)})
 
     def sum_copy(k, owner):
-        return remote(mine, samp_ref.at[owner], groups_y + k - 2, {"gy": peer(k)})
-
-    base = groups_y - 1
+        return remote(mine, samp_ref.at[owner], 1, {"gy": peer(k)})
+
+    def every(sem):
+        return pltpu.make_async_copy(gathered, gathered, sem)
+
+    base = 1
     chunk = cells_x // CHUNKS
 
     def y_copy(q, side):
@@ -312,8 +328,8 @@
         return remote(y_send.at[1 - side, :, :, rows, :], y_recv.at[side, :, :, rows, :],
                       2 * base + 2 + 2 * q + side, {"gy": south if side else north})
 
-    to_east = remote(field.at[:, cells_x - 1], x_recv.at[0], 2 * base, {"gx": tile_x + 1})
-    to_west = remote(field.at[:, 0], x_recv.at[1], 2 * base + 1, {"gx": tile_x - 1})
+    to_east = remote(field.at[:, :, cells_x - 1], x_recv.at[0], 2 * base, {"gx": tile_x + 1})
+    to_west = remote(field.at[:, :, 0], x_recv.at[1], 2 * base + 1, {"gx": tile_x - 1})
 
     for k in range(1, groups_y):
         part_copy(k).start()
@@ -338,11 +354,10 @@
     first_row, last_row = sub == 0, sub == 7
     first_lane, last_lane = lane == 0, lane == LANES - 1
     zero = jnp.zeros((8, LANES), F32)
-    halves = [pl.ds(half * LANES, LANES) for half in range(2)]
     strips = cells_y // 8
 
     def tile(c, i, t, half):
-        return field[c, i, pl.ds(8 * t, 8), halves[half]]
+        return field[half, c, i, pl.ds(8 * t, 8), :]
 
     def ghost(side, half, c, i):
         return y_recv[side, half, c, pl.ds(i, 8, stride=0), :]
@@ -360,32 +375,30 @@
             for half in range(2):
                 bu, bv, bw = (b * here[c][half] for c in range(3))
                 for c in range(comps):
+                    value = here[c][half]
                     if t > 0:
-                        below = pltpu.roll(tile(c, i, t - 1, half), 1, 0)
+                        to_s = field[half, c, i, pl.ds(8 * t - 1, 8), :]
                     else:
-                        below = zero
+                        to_s = jnp.where(first_row, zero, pltpu.roll(value, 1, 0))
                     if t < strips - 1:
-                        above = pltpu.roll(tile(c, i, t + 1, half), 7, 0)
+                        to_n = field[half, c, i, pl.ds(8 * t + 1, 8), :]
                     else:
-                        above = zero
-                    value = here[c][half]
-                    to_s = jnp.where(first_row, below, pltpu.roll(value, 1, 0))
-                    to_n = jnp.where(last_row, above, pltpu.roll(value, 7, 0))
+                        to_n = jnp.where(last_row, zero, pltpu.roll(value, 7, 0))
                     out = (
                         centre * value
-                        + ((a - bu) * east(c, rows, halves[half]) + (a + bu) * west(c, rows, halves[half]))
+                        + ((a - bu) * east(half, c, rows) + (a + bu) * west(half, c, rows))
                         + ((a - bv) * to_n + (a + bv) * to_s)
                         + ((a - bw) * upper[c][half] + (a + bw) * lower[c][half])
                     )
                     if second:
-                        out = out + 0.5 * old[c, i, rows, halves[half]]
-                    result[c, i, rows, halves[half]] = out
+                        out = out + 0.5 * old[half, c, i, rows, :]
+                    result[half, c, i, rows, :] = out
 
     def inside(i):
         plane(
             i,
-            lambda c, rows, lanes: field[c, i - 1, rows, lanes],
-            lambda c, rows, lanes: field[c, i + 1, rows, lanes],
+            lambda half, c, rows: field[half, c, i - 1, rows, :],
+            lambda half, c, rows: field[half, c, i + 1, rows, :],
         )
 
     def piece(start, stop):
@@ -398,8 +411,7 @@
     cuts = [1 + STEP * (steps * k // 4) for k in (0, 2, 4)]
 
     piece(cuts[0], cuts[1])
-    for k in range(1, groups_y):
-        part_copy(k).wait_recv()
+    every(recv_sem.at[0]).wait()
     total = functools.reduce(jnp.add, [gathered[k] for k in range(groups_y - 1)], part_ref[tile_y])
     mine[...] = total
     samp_ref[tile_y] = total
@@ -419,13 +431,13 @@
 
     plane(
         0,
-        lambda c, rows, lanes: x_recv[0, c, rows, lanes],
-        lambda c, rows, lanes: field[c, 1, rows, lanes],
+        lambda half, c, rows: x_recv[0, half, c, rows, :],
+        lambda half, c, rows: field[half, c, 1, rows, :],
     )
     plane(
         cells_x - 1,
-        lambda c, rows, lanes: field[c, cells_x - 2, rows, lanes],
-        lambda c, rows, lanes: x_recv[1, c, rows, lanes],
+        lambda half, c, rows: field[half, c, cells_x - 2, rows, :],
+        lambda half, c, rows: x_recv[1, half, c, rows, :],
     )
 
     for q in range(CHUNKS):
@@ -442,14 +454,12 @@
                         bv = b * tile(1, i, t, half)
                         weight = jnp.where(mask, a - bv if side else a + bv, 0.0)
                         for c in range(comps):
-                            before = result[c, i, rows, halves[half]]
-                            result[c, i, rows, halves[half]] = before + weight * ghost(side, half, c, i)
-
-    for k in range(1, groups_y):
-        sum_copy(k, peer(groups_y - k)).wait_recv()
-    for k in range(1, groups_y):
-        part_copy(k).wait_send()
-        sum_copy(k, tile_y).wait_send()
+                            before = result[half, c, i, rows, :]
+                            result[half, c, i, rows, :] = before + weight * ghost(side, half, c, i)
+
+    every(recv_sem.at[1]).wait()
+    every(send_sem.at[0]).wait()
+    every(send_sem.at[1]).wait()
     for q in range(CHUNKS):
         for side in range(2):
             y_copy(q, side).wait_send()
@@ -471,7 +481,7 @@
     velocity, pos, tiles = (
         pltpu.with_memory_space_constraint(x, pltpu.HBM) for x in (velocity, pos, tiles)
     )
-    grid = pltpu.VMEM(velocity.shape, F32)
+    grid = pltpu.VMEM((2, comps, cells_x, cells_y, LANES), F32)
     table = pltpu.VMEM((groups_y, comps, recs * points // (groups_y * LANES), LANES), F32)
 
     field, _, part, plan, picks, here = pl.pallas_call(
@@ -489,14 +499,14 @@
         scratch_shapes=[
             pltpu.VMEM(tiles.shape, I32),
             pltpu.VMEM((8, LANES), I32),
-            pltpu.SemaphoreType.DMA((CHUNKS + 3,)),
+            pltpu.SemaphoreType.DMA((2 * CHUNKS + 3,)),
         ],
         compiler_params=params(),
         name="sample_first",
     )(velocity, pos, tiles, counts)
 
     def swap(second, *operands):
-        sems = 2 * (groups_y - 1) + 2 + 2 * CHUNKS
+        sems = 4 + 2 * CHUNKS
         return pl.pallas_call(
             functools.partial(exchange, groups_x, groups_y, second),
             out_shape=(grid, table),
@@ -505,7 +515,7 @@
             scratch_shapes=[
                 pltpu.VMEM((2, 2, comps, cells_x, LANES), F32),
                 pltpu.VMEM((2, 2, comps, cells_x, LANES), F32),
-                pltpu.VMEM((2, comps, cells_y, depth), F32),
+                pltpu.VMEM((2, 2, comps, cells_y, LANES), F32),
                 pltpu.VMEM((groups_y - 1, *table.shape[1:]), F32),
                 pltpu.VMEM(table.shape[1:], F32),
                 pltpu.SemaphoreType.DMA((sems,)),
@@ -536,7 +546,7 @@
         in_specs=[SMEM, VMEM, VMEM, VMEM, SMEM, VMEM, VMEM, VMEM],
         out_specs=(VMEM, HBM, HBM),
         input_output_aliases={7: 0},
-        scratch_shapes=[pltpu.VMEM(pos.shape, F32), pltpu.SemaphoreType.DMA((CHUNKS + 1,))],
+        scratch_shapes=[pltpu.VMEM(pos.shape, F32), pltpu.SemaphoreType.DMA((2 * CHUNKS + 1,))],
         compiler_params=params(),
         name="spread_last",
     )(plan, picks, here, coefs, counts, samp_a, samp_b, final)

time: 58.5 us -> 56.1 us (0.959)
  the two profiles are of different devices: /device:TPU:16 before, /device:TPU:1 now
where the time goes in v6:
time: 56.1 us; the launch traced here: 55.5 us
  Pallas kernels  54.1 us (96%)
  between operations  1.37 us (2%)
    pallas_call x2, Pallas kernels, swap(): pl.pallas_call(functools.partial(exchange, groups_x, groups_y, second), o...  44 us
    pallas_call x1, Pallas kernels, local(): pl.pallas_call(functools.partial(sample_first, total_y, groups_y), out_sh...  5.23 us
    pallas_call x1, Pallas kernels, local(): pl.pallas_call(spread_last, out_shape=(grid, jax.ShapeDtypeStruct(velocit...  3.87 us

profile of v6, /device:TPU:1, one launch (start us, length us, event | category | flops | bytes accessed | tf_op | source)
XLA Modules:
  0.0 55.5 jit_solution(14412166068668552073)
XLA Ops:
  0.6 0.0 copy-start
  1.3 0.0 copy-start.1
  1.3 5.2 %sample_first.1 = (f32[2,3,96,32,128]{4,3,2,1,0:T(8,128)S(1)}, s32[3,64,256]{2,1,0:T(8,128)}, f32[16,3,8,128]{3,2,1,0:T(8,128)S(1)}, s32[8,128]{1,0:T(8,128)S(4)...) custom-call(f32[3,96,32,256]{3,2,1,0:T(8,128)} %vel_hbm.1, s32[3,64,256]{2,1,0:T(8,128)} %bitcast.12, ...), custom_call_target="tpu_custom_call" | custom-call | tf_op jit(solution)/shard_map/sample_first/pallas_call | solution.py:487
  6.6 0.0 copy-done
  6.6 21.7 %exchange_first.1 = (f32[2,3,96,32,128]{4,3,2,1,0:T(8,128)S(1)}, f32[16,3,8,128]{3,2,1,0:T(8,128)S(1)}) custom-call(f32[2,3,96,32,128]{4,3,2,1,0:T(8,128)S(1)} %get-tuple-element.18.refs_0_, f32[16,3,8,128]{3,2,1,0:T(8,128)S(1)} %get-tuple-element.19.refs_1_, f32[3,32,256]{2,1,0:T(8,128)S(1)} %copy-done), custom_call_target="tpu_custom_call" | custom-call | tf_op jit(solution)/shard_map/exchange_first/pallas_call | solution.py:510
  28.3 0.0 copy-done.1
  28.3 1.0 %spread_and_sample.1 = (f32[2,3,96,32,128]{4,3,2,1,0:T(8,128)S(1)}, f32[16,3,8,128]{3,2,1,0:T(8,128)S(1)}) custom-call(s32[8,128]{1,0:T(8,128)S(4)} %get-tuple-element.15.plan_ref, bf16[64,256,256]{2,1,0:T(8,128)(2,1)S(1)} %get-tuple-element.16.pick_ref, s32[64,256]{1,0:T(8,128)S(1)} %get-tuple-element.17.here_ref, ...), custom_call_target="tpu_custom_call", output_to_operand_aliasing={{0}: (5, {})} | custom-call | tf_op jit(solution)/shard_map/spread_and_sample/pallas_call | solution.py:529
  29.3 22.3 %exchange_second.1 = (f32[2,3,96,32,128]{4,3,2,1,0:T(8,128)S(1)}, f32[16,3,8,128]{3,2,1,0:T(8,128)S(1)}) custom-call(f32[2,3,96,32,128]{4,3,2,1,0:T(8,128)S(1)} %get-tuple-element.18.refs_0_, f32[2,3,96,32,128]{4,3,2,1,0:T(8,128)S(1)} %get-tuple-element.22.refs_1_, f32[16,3,8,128]{3,2,1,0:T(8,128)S(1)} %get-tuple-element.23.refs_2_, f32[3,32,256]{2,1,0:T(8,128)S(1)} %copy-done), custom_call_target="tpu_custom_call" | custom-call | tf_op jit(solution)/shard_map/exchange_second/pallas_call | solution.py:510
  51.6 3.9 %spread_last.1 = (f32[2,3,96,32,128]{4,3,2,1,0:T(8,128)S(1)}, f32[3,96,32,256]{3,2,1,0:T(8,128)}, f32[3,64,256]{2,1,0:T(8,128)}) custom-call(s32[8,128]{1,0:T(8,128)S(4)} %get-tuple-element.15.plan_ref, bf16[64,256,256]{2,1,0:T(8,128)(2,1)S(1)} %get-tuple-element.16.pick_ref, ...), custom_call_target="tpu_custom_call", output_to_operand_aliasing={{0}: (7, {})} | custom-call | tf_op jit(solution)/shard_map/spread_last/pallas_call | solution.py:539
Async XLA Ops:
  0.6 5.9 %copy-start = (f32[3,32,256]{2,1,0:T(8,128)S(1)}, f32[3,32,256]{2,1,0:T(8,128)}, u32[]{:S(2)}) copy-start(f32[3,32,256]{2,1,0:T(8,128)} %refs_3_.1) | copy-start | bytes 294916
  1.3 26.9 %copy-start.1 = (f32[1,64,256]{2,1,0:T(8,128)S(1)}, f32[1,64,256]{2,1,0:T(8,128)}, u32[]{:S(2)}) copy-start(f32[1,64,256]{2,1,0:T(8,128)} %param.10) | copy-start | bytes 196612

commit v7 on v6

--- a/solution.py
+++ b/solution.py
@@ -21,7 +21,7 @@
 SMEM = pl.BlockSpec(memory_space=pltpu.SMEM)
 HBM = pl.BlockSpec(memory_space=pltpu.HBM)
 LANES = 128
-GROUP = 4
+GROUP, SMALL = 8, 4
 STEP = 4
 CHUNKS = 4
 
@@ -143,6 +143,12 @@
     rows_ref[1:2, :] = jnp.sum(jnp.where(mine, hub, 0).astype(F32), axis=0, keepdims=True).astype(I32)
     below = active & (hub < lane)
     rows_ref[2:3, :] = jnp.sum(below.astype(F32), axis=0, keepdims=True).astype(I32)
+
+
+def over_records(count, step):
+    full = count // GROUP
+    pl.loop(0, full)(step(GROUP))
+    pl.loop(full * (GROUP // SMALL), (count + SMALL - 1) // SMALL)(step(SMALL))
 
 
 def sample_first(total_y, groups_y, vel_hbm, pos_hbm, tiles_hbm, counts_ref,
@@ -183,14 +189,9 @@
 
         return body
 
-    start = jnp.int32(0)
-    for q in range(CHUNKS):
-        loads[2 * q].wait()
-        loads[2 * q + 1].wait()
-        stop = (count if q == CHUNKS - 1 else plan_ref[2, (q + 1) * chunk - RAD]) // GROUP
-        pl.loop(start, stop)(sample(GROUP))
-        start = stop
-    pl.loop(start * (GROUP // 2), (count + 1) // 2)(sample(2))
+    for load in loads:
+        load.wait()
+    over_records(count, sample)
 
 
 def spread_and_sample(plan_ref, pick_ref, here_ref, coef_ref, samp_ref, _, field, part_ref):
@@ -210,10 +211,8 @@
 
         return body
 
-    full = count // GROUP
-    for step in (spread, sample):
-        pl.loop(0, full)(step(GROUP))
-        pl.loop(full * (GROUP // 2), (count + 1) // 2)(step(2))
+    over_records(count, spread)
+    over_records(count, sample)
 
 
 def spread_last(plan_ref, pick_ref, here_ref, coef_ref, counts_ref, samp_a, samp_b, _,
@@ -235,28 +234,36 @@
                 blade[c, rows, lanes] = strength * (speed_a * a[c] + speed_b * b[c])
     put = pltpu.make_async_copy(blade, blade_hbm, sems.at[2 * CHUNKS])
     put.start()
-    start = jnp.int32(0)
-    stores = []
+    full = count // GROUP
+
+    def spread(size):
+        def body(at):
+            spread_group(size, field, plan_ref, pick_ref, here_ref, coef_ref, samp_b,
+                         0.5 * TIME_STEP, at, count)
+
+        return body
+
+    def store(q, half):
+        planes, lanes = pl.ds(q * chunk, chunk), pl.ds(half * LANES, LANES)
+        return pltpu.make_async_copy(
+            field.at[half, :, planes], next_hbm.at[:, planes, :, lanes], sems.at[2 * q + half]
+        )
+
+    def finish(q, done):
+        large, small = done
+        upto = jnp.where(q == CHUNKS - 1, count, plan_ref[2, (q + 1) * chunk + RAD])
+        large_stop = jnp.minimum((upto + GROUP - 1) // GROUP, full)
+        small_stop = jnp.maximum((upto + SMALL - 1) // SMALL, small)
+        pl.loop(large, large_stop)(spread(GROUP))
+        pl.loop(small, small_stop)(spread(SMALL))
+        for half in range(2):
+            store(q, half).start()
+        return large_stop, small_stop
+
+    lax.fori_loop(0, CHUNKS, finish, (jnp.int32(0), full * (GROUP // SMALL)))
     for q in range(CHUNKS):
-        upto = count if q == CHUNKS - 1 else plan_ref[2, (q + 1) * chunk + RAD]
-        stop = (upto + GROUP - 1) // GROUP
-
-        @pl.loop(start, stop)
-        def _(at):
-            spread_group(GROUP, field, plan_ref, pick_ref, here_ref, coef_ref, samp_b,
-                         0.5 * TIME_STEP, at, count)
-
-        planes = pl.ds(q * chunk, chunk)
         for half in range(2):
-            lanes = pl.ds(half * LANES, LANES)
-            stores.append(pltpu.make_async_copy(
-                field.at[half, :, planes], next_hbm.at[:, planes, :, lanes], sems.at[2 * q + half]
-            ))
-            stores[-1].start()
-        start = stop
-
-    for store in stores:
-        store.wait()
+            store(q, half).wait()
     put.wait()
 
 
@@ -333,7 +340,7 @@
 
     for k in range(1, groups_y):
         part_copy(k).start()
-    for q in range(CHUNKS):
+    for q in range(CHUNKS - 1):
         for side in range(2):
             y_copy(q, side).start()
 
@@ -417,6 +424,9 @@
     samp_ref[tile_y] = total
     for k in range(1, groups_y):
         sum_copy(k, tile_y).start()
+    for q in (CHUNKS - 1,):
+        for side in range(2):
+            y_copy(q, side).start()
     piece(cuts[1], cuts[2])
     for i in range(cuts[2], cells_x - 1):
         inside(i)

time: 56.1 us -> 55.8 us (level)
  the two profiles are of different devices: /device:TPU:1 before, /device:TPU:20 now
where the time goes in v7:
time: 55.8 us; the launch traced here: 55.6 us
  Pallas kernels  54.2 us (97%)
  between operations  1.37 us (2%)
    pallas_call x2, Pallas kernels, swap(): pl.pallas_call(functools.partial(exchange, groups_x, groups_y, second), o...  32.2 us
    pallas_call x1, Pallas kernels, local(): pl.pallas_call(functools.partial(sample_first, total_y, groups_y), out_sh...  8.3 us
    pallas_call x1, Pallas kernels, local(): pl.pallas_call(spread_and_sample, out_shape=(grid, table), in_specs=[SMEM...  7.76 us
    pallas_call x1, Pallas kernels, local(): pl.pallas_call(spread_last, out_shape=(grid, jax.ShapeDtypeStruct(velocit...  5.95 us

profile of v7, /device:TPU:20, one launch (start us, length us, event | category | flops | bytes accessed | tf_op | source)
XLA Modules:
  0.0 55.6 jit_solution(11822742230807350138)
XLA Ops:
  0.6 0.0 copy-start
  1.3 0.0 copy-start.1
  1.3 8.3 %sample_first.1 = (f32[2,3,96,32,128]{4,3,2,1,0:T(8,128)S(1)}, s32[3,64,256]{2,1,0:T(8,128)}, f32[16,3,8,128]{3,2,1,0:T(8,128)S(1)}, s32[8,128]{1,0:T(8,128)S(4)...) custom-call(f32[3,96,32,256]{3,2,1,0:T(8,128)} %vel_hbm.1, s32[3,64,256]{2,1,0:T(8,128)} %bitcast.12, ...), custom_call_target="tpu_custom_call" | custom-call | tf_op jit(solution)/shard_map/sample_first/pallas_call | solution.py:497
  9.6 0.0 copy-done
  9.7 16.4 %exchange_first.1 = (f32[2,3,96,32,128]{4,3,2,1,0:T(8,128)S(1)}, f32[16,3,8,128]{3,2,1,0:T(8,128)S(1)}) custom-call(f32[2,3,96,32,128]{4,3,2,1,0:T(8,128)S(1)} %get-tuple-element.18.refs_0_, f32[16,3,8,128]{3,2,1,0:T(8,128)S(1)} %get-tuple-element.19.refs_1_, f32[3,32,256]{2,1,0:T(8,128)S(1)} %copy-done), custom_call_target="tpu_custom_call" | custom-call | tf_op jit(solution)/shard_map/exchange_first/pallas_call | solution.py:520
  26.0 0.0 copy-done.1
  26.1 7.8 %spread_and_sample.1 = (f32[2,3,96,32,128]{4,3,2,1,0:T(8,128)S(1)}, f32[16,3,8,128]{3,2,1,0:T(8,128)S(1)}) custom-call(s32[8,128]{1,0:T(8,128)S(4)} %get-tuple-element.15.plan_ref, bf16[64,256,256]{2,1,0:T(8,128)(2,1)S(1)} %get-tuple-element.16.pick_ref, s32[64,256]{1,0:T(8,128)S(1)} %get-tuple-element.17.here_ref, ...), custom_call_target="tpu_custom_call", output_to_operand_aliasing={{0}: (5, {})} | custom-call | tf_op jit(solution)/shard_map/spread_and_sample/pallas_call | solution.py:539
  33.8 15.9 %exchange_second.1 = (f32[2,3,96,32,128]{4,3,2,1,0:T(8,128)S(1)}, f32[16,3,8,128]{3,2,1,0:T(8,128)S(1)}) custom-call(f32[2,3,96,32,128]{4,3,2,1,0:T(8,128)S(1)} %get-tuple-element.18.refs_0_, f32[2,3,96,32,128]{4,3,2,1,0:T(8,128)S(1)} %get-tuple-element.22.refs_1_, f32[16,3,8,128]{3,2,1,0:T(8,128)S(1)} %get-tuple-element.23.refs_2_, f32[3,32,256]{2,1,0:T(8,128)S(1)} %copy-done), custom_call_target="tpu_custom_call" | custom-call | tf_op jit(solution)/shard_map/exchange_second/pallas_call | solution.py:520
  49.7 5.9 %spread_last.1 = (f32[2,3,96,32,128]{4,3,2,1,0:T(8,128)S(1)}, f32[3,96,32,256]{3,2,1,0:T(8,128)}, f32[3,64,256]{2,1,0:T(8,128)}) custom-call(s32[8,128]{1,0:T(8,128)S(4)} %get-tuple-element.15.plan_ref, bf16[64,256,256]{2,1,0:T(8,128)(2,1)S(1)} %get-tuple-element.16.pick_ref, ...), custom_call_target="tpu_custom_call", output_to_operand_aliasing={{0}: (7, {})} | custom-call | tf_op jit(solution)/shard_map/spread_last/pallas_call | solution.py:549
Async XLA Ops:
  0.6 9.0 %copy-start = (f32[3,32,256]{2,1,0:T(8,128)S(1)}, f32[3,32,256]{2,1,0:T(8,128)}, u32[]{:S(2)}) copy-start(f32[3,32,256]{2,1,0:T(8,128)} %refs_3_.1) | copy-start | bytes 294916
  1.3 24.7 %copy-start.1 = (f32[1,64,256]{2,1,0:T(8,128)S(1)}, f32[1,64,256]{2,1,0:T(8,128)}, u32[]{:S(2)}) copy-start(f32[1,64,256]{2,1,0:T(8,128)} %param.10) | copy-start | bytes 196612

commit v8 on v7

--- a/solution.py
+++ b/solution.py
@@ -160,15 +160,16 @@
     fetch_tiles = pltpu.make_async_copy(tiles_hbm, tiles_ref, sems.at[2 * CHUNKS + 1])
     fetch_pos.start()
     fetch_tiles.start()
-    loads = []
+
+    def load(q, half):
+        planes, lanes = pl.ds(q * chunk, chunk), pl.ds(half * LANES, LANES)
+        return pltpu.make_async_copy(
+            vel_hbm.at[:, planes, :, lanes], field.at[half, :, planes], sems.at[2 * q + half]
+        )
+
     for q in range(CHUNKS):
-        planes = pl.ds(q * chunk, chunk)
-        for half in range(2):
-            lanes = pl.ds(half * LANES, LANES)
-            loads.append(pltpu.make_async_copy(
-                vel_hbm.at[:, planes, :, lanes], field.at[half, :, planes], sems.at[2 * q + half]
-            ))
-            loads[-1].start()
+        for half in range(2):
+            load(q, half).start()
     part_ref[...] = jnp.zeros_like(part_ref)
     rows_ref[...] = jnp.zeros_like(rows_ref)
     fetch_pos.wait()
@@ -189,9 +190,16 @@
 
         return body
 
-    for load in loads:
-        load.wait()
-    over_records(count, sample)
+    def ready(q, start):
+        for half in range(2):
+            load(q, half).wait()
+        upto = jnp.where(q == CHUNKS - 1, count, plan_ref[2, (q + 1) * chunk - RAD])
+        stop = upto // GROUP
+        pl.loop(start, stop)(sample(GROUP))
+        return stop
+
+    full = lax.fori_loop(0, CHUNKS, ready, jnp.int32(0))
+    pl.loop(full * (GROUP // SMALL), (count + SMALL - 1) // SMALL)(sample(SMALL))
 
 
 def spread_and_sample(plan_ref, pick_ref, here_ref, coef_ref, samp_ref, _, field, part_ref):

time: 55.8 us -> 56.2 us (level)
  the two profiles are of different devices: /device:TPU:20 before, /device:TPU:24 now
where the time goes in v8:
time: 56.2 us; the launch traced here: 57.1 us
  Pallas kernels  55.7 us (99%)
  between operations  1.37 us (2%)
    pallas_call x2, Pallas kernels, swap(): pl.pallas_call(functools.partial(exchange, groups_x, groups_y, second), o...  34.9 us
    pallas_call x1, Pallas kernels, local(): pl.pallas_call(spread_and_sample, out_shape=(grid, table), in_specs=[SMEM...  7.75 us
    pallas_call x1, Pallas kernels, local(): pl.pallas_call(functools.partial(sample_first, total_y, groups_y), out_sh...  7.12 us
    pallas_call x1, Pallas kernels, local(): pl.pallas_call(spread_last, out_shape=(grid, jax.ShapeDtypeStruct(velocit...  5.95 us

profile of v8, /device:TPU:24, one launch (start us, length us, event | category | flops | bytes accessed | tf_op | source)
XLA Modules:
  0.0 57.1 jit_solution(12419989295867817348)
XLA Ops:
  0.6 0.0 copy-start
  1.3 0.0 copy-start.1
  1.3 7.1 %sample_first.1 = (f32[2,3,96,32,128]{4,3,2,1,0:T(8,128)S(1)}, s32[3,64,256]{2,1,0:T(8,128)}, f32[16,3,8,128]{3,2,1,0:T(8,128)S(1)}, s32[8,128]{1,0:T(8,128)S(4)...) custom-call(f32[3,96,32,256]{3,2,1,0:T(8,128)} %vel_hbm.1, s32[3,64,256]{2,1,0:T(8,128)} %bitcast.12, ...), custom_call_target="tpu_custom_call" | custom-call | tf_op jit(solution)/shard_map/sample_first/pallas_call | solution.py:505
  8.5 0.0 copy-done
  8.5 19.0 %exchange_first.1 = (f32[2,3,96,32,128]{4,3,2,1,0:T(8,128)S(1)}, f32[16,3,8,128]{3,2,1,0:T(8,128)S(1)}) custom-call(f32[2,3,96,32,128]{4,3,2,1,0:T(8,128)S(1)} %get-tuple-element.18.refs_0_, f32[16,3,8,128]{3,2,1,0:T(8,128)S(1)} %get-tuple-element.19.refs_1_, f32[3,32,256]{2,1,0:T(8,128)S(1)} %copy-done), custom_call_target="tpu_custom_call" | custom-call | tf_op jit(solution)/shard_map/exchange_first/pallas_call | solution.py:528
  27.5 0.0 copy-done.1
  27.5 7.7 %spread_and_sample.1 = (f32[2,3,96,32,128]{4,3,2,1,0:T(8,128)S(1)}, f32[16,3,8,128]{3,2,1,0:T(8,128)S(1)}) custom-call(s32[8,128]{1,0:T(8,128)S(4)} %get-tuple-element.15.plan_ref, bf16[64,256,256]{2,1,0:T(8,128)(2,1)S(1)} %get-tuple-element.16.pick_ref, s32[64,256]{1,0:T(8,128)S(1)} %get-tuple-element.17.here_ref, ...), custom_call_target="tpu_custom_call", output_to_operand_aliasing={{0}: (5, {})} | custom-call | tf_op jit(solution)/shard_map/spread_and_sample/pallas_call | solution.py:547
  35.3 15.8 %exchange_second.1 = (f32[2,3,96,32,128]{4,3,2,1,0:T(8,128)S(1)}, f32[16,3,8,128]{3,2,1,0:T(8,128)S(1)}) custom-call(f32[2,3,96,32,128]{4,3,2,1,0:T(8,128)S(1)} %get-tuple-element.18.refs_0_, f32[2,3,96,32,128]{4,3,2,1,0:T(8,128)S(1)} %get-tuple-element.22.refs_1_, f32[16,3,8,128]{3,2,1,0:T(8,128)S(1)} %get-tuple-element.23.refs_2_, f32[3,32,256]{2,1,0:T(8,128)S(1)} %copy-done), custom_call_target="tpu_custom_call" | custom-call | tf_op jit(solution)/shard_map/exchange_second/pallas_call | solution.py:528
  51.1 5.9 %spread_last.1 = (f32[2,3,96,32,128]{4,3,2,1,0:T(8,128)S(1)}, f32[3,96,32,256]{3,2,1,0:T(8,128)}, f32[3,64,256]{2,1,0:T(8,128)}) custom-call(s32[8,128]{1,0:T(8,128)S(4)} %get-tuple-element.15.plan_ref, bf16[64,256,256]{2,1,0:T(8,128)(2,1)S(1)} %get-tuple-element.16.pick_ref, ...), custom_call_target="tpu_custom_call", output_to_operand_aliasing={{0}: (7, {})} | custom-call | tf_op jit(solution)/shard_map/spread_last/pallas_call | solution.py:557
Async XLA Ops:
  0.6 7.8 %copy-start = (f32[3,32,256]{2,1,0:T(8,128)S(1)}, f32[3,32,256]{2,1,0:T(8,128)}, u32[]{:S(2)}) copy-start(f32[3,32,256]{2,1,0:T(8,128)} %refs_3_.1) | copy-start | bytes 294916
  1.3 26.2 %copy-start.1 = (f32[1,64,256]{2,1,0:T(8,128)S(1)}, f32[1,64,256]{2,1,0:T(8,128)}, u32[]{:S(2)}) copy-start(f32[1,64,256]{2,1,0:T(8,128)} %param.10) | copy-start | bytes 196612
